TPU v7x, 512 devices: a whole 4x4x16 slice. The times are simulated.
512 devices in a mesh: sector: 64 (over x, z), mpo: 8 (over y, core).
Axes of the slice: x: 4, y: 4, z: 16, core: 2. Of those that a mesh axis runs over, the one named last changes fastest.
Arguments:
- wavefunction: bfloat16 [64, 512, 512], P('sector'), may hold values from -6 to 6
- left_environment: bfloat16 [32, 64, 512, 512], P('mpo', 'sector'), may hold values from -0.25 to 0.25
- right_environment: bfloat16 [32, 64, 512, 512], P('mpo', 'sector'), may hold values from -0.25 to 0.25
- term_shift: int32 [32], P('mpo'), may hold values from 0 to 4, as said below
- coupling: float32 [32], P('mpo'), may hold values from 0.1 to 0.4
- block_sizes: int32 [64], P('sector'), may hold values from 128 to 512
Outputs:
- applied: float32 [64, 512, 512], P('sector', 'mpo')
Inputs may be any that keep to these rules, and one draw needn't show every extreme that they name: `term_shift`: each of the five codes is held by some MPO index.
All inputs are finite; a program needn't handle non-finite values.
Results may differ from a plain program's by a relative error of at most 0.0003.
Values may be sent and summed in bfloat16 or wider, within the bound.
No kernel may reach another device: no remote copies, remote signals or barrier semaphores. Data moves between devices by JAX's collectives and lax.ppermute only.
A program may use at most 64 MiB of HBM per device.

v0:
```python
import jax
import jax.numpy as jnp
from jax import lax
from jax.sharding import PartitionSpec as P

GRID = 8


def shifted(block, axis, distance):
    devices = range(lax.axis_size(axis))
    route = [(i - distance, i) for i in devices if i - distance in devices]
    return lax.ppermute(block, axis, route)


def per_device(
    wavefunction, left_environment, right_environment, term_shift, coupling, block_sizes
):
    extent = wavefunction.shape[1]
    positions = jnp.arange(extent)
    live = positions < block_sizes[0]
    block_mask = live[:, None] & live[None, :]
    masked = jnp.where(block_mask, wavefunction[0], jnp.zeros_like(wavefunction[0]))
    lower = shifted(masked, "sector", 1)
    higher = shifted(masked, "sector", -1)
    below = shifted(masked, "sector", GRID)
    above = shifted(masked, "sector", -GRID)
    candidates = jnp.stack([masked, lower, higher, below, above])
    selected = jnp.take(candidates, term_shift, axis=0)
    left_local = left_environment[:, 0]
    right_wide = right_environment[:, 0].astype(jnp.float32)
    share = extent // lax.axis_size("mpo")
    partial_left = jnp.einsum(
        "wij,wjk->wik", left_local, selected, preferred_element_type=jnp.float32
    )
    products = jnp.einsum("wik,wlk->wil", partial_left, right_wide, precision=lax.Precision.HIGHEST)
    weighted = jnp.sum(coupling[:, None, None] * products, axis=0)
    total = lax.psum(jnp.where(block_mask, weighted, jnp.zeros_like(weighted)), "mpo")
    mine = lax.dynamic_slice_in_dim(total, lax.axis_index("mpo") * share, share, 0)
    return mine[None]


def solution(mesh):
    placed = (
        P("sector", None, None),
        P("mpo", "sector", None, None),
        P("mpo", "sector", None, None),
        P("mpo"),
        P("mpo"),
        P("sector"),
    )
    return jax.shard_map(
        per_device, mesh=mesh, in_specs=placed, out_specs=P("sector", "mpo", None), check_vma=False
    )
```

profile of v0, /device:TPU:2, one launch (start us, length us, event | category | flops | bytes accessed | tf_op | source)
XLA Modules:
  0.0 223.5 jit_solution(15033826622319398422)
XLA Ops:
  6.5 0.0 copy-start
  7.4 1.3 and_select_fusion.1
  8.6 3.8 %collective-permute-start = (bf16[512,512]{1,0:T(8,128)(2,1)S(1)}, bf16[512,512]{1,0:T(8,128)(2,1)S(1)}, u32[]{:S(2)}, u32[]{:S(2)}) collective-permute-start(bf16[512,512]{1,0:T(8,128)(2,1)S(1)} %and_select_fusion.1), channel_id=1, source_target_pairs={{0,8},{8,16},{16,24},{24,32},{32,40},{40,48},{48,56},{56,64},{64,7... | collective-permute-start | bytes 1572872 | tf_op jit(solution)/shard_map/ppermute | solution.py:12
  12.5 9.5 %collective-permute-start.1 = (bf16[512,512]{1,0:T(8,128)(2,1)S(1)}, bf16[512,512]{1,0:T(8,128)(2,1)S(1)}, u32[]{:S(2)}, u32[]{:S(2)}) collective-permute-start(bf16[512,512]{1,0:T(8,128)(2,1)S(1)} %and_select_fusion.1), channel_id=1, source_target_pairs={{8,0},{16,8},{24,16},{32,24},{40,32},{48,40},{56,48},{64,56},{72,6... | collective-permute-start | bytes 1572872 | tf_op jit(solution)/shard_map/ppermute | solution.py:12
  21.9 9.5 %collective-permute-start.2 = (bf16[512,512]{1,0:T(8,128)(2,1)S(1)}, bf16[512,512]{1,0:T(8,128)(2,1)S(1)}, u32[]{:S(2)}, u32[]{:S(2)}) collective-permute-start(bf16[512,512]{1,0:T(8,128)(2,1)S(1)} %and_select_fusion.1), channel_id=1, source_target_pairs={{0,64},{8,72},{16,80},{24,88},{32,96},{40,104},{48,112},{56,120},{... | collective-permute-start | bytes 1572872 | tf_op jit(solution)/shard_map/ppermute | solution.py:12
  31.4 6.0 %collective-permute-start.3 = (bf16[512,512]{1,0:T(8,128)(2,1)S(1)}, bf16[512,512]{1,0:T(8,128)(2,1)S(1)}, u32[]{:S(2)}, u32[]{:S(2)}) collective-permute-start(bf16[512,512]{1,0:T(8,128)(2,1)S(1)} %and_select_fusion.1), channel_id=1, source_target_pairs={{64,0},{72,8},{80,16},{88,24},{96,32},{104,40},{112,48},{120,56},{... | collective-permute-start | bytes 1572872 | tf_op jit(solution)/shard_map/ppermute | solution.py:12
  37.4 2.1 fusion.6
  39.5 0.7 compare_select_fusion
  40.1 0.7 compare_and_fusion
  40.8 0.0 collective-permute-done
  40.8 0.8 bitcast_dynamic-update-slice_fusion.3
  41.6 61.5 %collective-permute-done.1 = bf16[512,512]{1,0:T(8,128)(2,1)S(1)} collective-permute-done((bf16[512,512]{1,0:T(8,128)(2,1)S(1)}, bf16[512,512]{1,0:T(8,128)(2,1)S(1)}, u32[]{:S(2)}, u32[]{:S(2)}) %collective-permute-start.1) | collective-permute-done | bytes 524320 | tf_op jit(solution)/shard_map/ppermute | solution.py:12
  103.1 0.8 bitcast_dynamic-update-slice_fusion.2
  104.0 6.0 %collective-permute-done.2 = bf16[512,512]{1,0:T(8,128)(2,1)S(1)} collective-permute-done((bf16[512,512]{1,0:T(8,128)(2,1)S(1)}, bf16[512,512]{1,0:T(8,128)(2,1)S(1)}, u32[]{:S(2)}, u32[]{:S(2)}) %collective-permute-start.2) | collective-permute-done | bytes 524320 | tf_op jit(solution)/shard_map/ppermute | solution.py:12
  110.0 0.8 bitcast_dynamic-update-slice_fusion.1
  110.8 16.0 %collective-permute-done.3 = bf16[512,512]{1,0:T(8,128)(2,1)S(1)} collective-permute-done((bf16[512,512]{1,0:T(8,128)(2,1)S(1)}, bf16[512,512]{1,0:T(8,128)(2,1)S(1)}, u32[]{:S(2)}, u32[]{:S(2)}) %collective-permute-start.3) | collective-permute-done | bytes 524320 | tf_op jit(solution)/shard_map/ppermute | solution.py:12
  126.9 0.8 bitcast_dynamic-update-slice_fusion
  127.7 3.7 %gather_fusion = bf16[4,512,512]{2,1,0:T(8,128)(2,1)} fusion(bf16[5,512,512]{2,1,0:T(8,128)(2,1)} %bitcast_dynamic-update-slice_fusion, s32[1024]{0:T(1024)S(1)} %pad_clamp_fusion), kind=kCustom, calls=%fused_computation | custom fusion | bytes 4194320 | tf_op jit(solution)/shard_map/jit(_take)/gather | solution.py:28
  131.4 3.1 %fusion.1 = f32[4,512,512]{1,2,0:T(8,128)S(1)} fusion(bf16[4,1,512,512]{3,2,1,0:T(8,128)(2,1)S(1)} %copy-done, bf16[4,512,512]{2,1,0:T(8,128)(2,1)} %gather_fusion, pred[4]{0:T(512)(128)(4,1)S(1)} %compare_and_fusion), kind=kOutput, calls=%fused_computation.3 | convolution fusion | flops 1074790400 | bytes 8388612 | tf_op jit(solution)/shard_map/wij,wjk->wik/dot_general | solution.py:32
  134.6 4.0 %multiply_reduce_fusion = f32[512,512]{1,0:T(8,128)S(1)} fusion(f32[4,512,512]{1,2,0:T(8,128)S(1)} %fusion.1, bf16[4,1,512,512]{3,2,1,0:T(8,128)(2,1)S(1)} %copy-done.1, f32[4]{0:T(128)S(1)} %copy-done.2), kind=kOutput, calls=%fused_computation.1 | convolution fusion | flops 6444285952 | bytes 7340048 | tf_op jit(solution)/shard_map/wik,wlk->wil/dot_general | solution.py:35
  138.5 1.2 and_select_fusion
  139.7 0.0 all-reduce.2.cloned.1.call-update
  139.8 75.4 %all-reduce.2.cloned.1.call-done = f32[512,512]{1,0:T(8,128)} async-done(((f32[512,512]{1,0:T(8,128)}), f32[512,512]{1,0:T(8,128)}) %all-reduce.2.cloned.1.call-update) | async-done | bytes 1048592 | tf_op jit(solution)/shard_map/psum | solution.py:37
  215.1 1.6 dynamic-slice_bitcast_fusion
  (8 shorter events, 0.0 us)
Async XLA Ops:
  6.5 124.9 %copy-start = (bf16[4,1,512,512]{3,2,1,0:T(8,128)(2,1)S(1)}, bf16[4,1,512,512]{3,2,1,0:T(8,128)(2,1)}, u32[]{:S(2)}) copy-start(bf16[4,1,512,512]{3,2,1,0:T(8,128)(2,1)} %param.7) | copy-start | bytes 6291460
  6.5 208.6 %all-reduce.2.cloned.1.call-start = ((), (), s32[]{:S(2)}) async-start(), calls=%async_computation | async-start | bytes 2097152 | tf_op jit(solution)/shard_map/psum | solution.py:37
  8.6 32.2 %collective-permute-start = (bf16[512,512]{1,0:T(8,128)(2,1)S(1)}, bf16[512,512]{1,0:T(8,128)(2,1)S(1)}, u32[]{:S(2)}, u32[]{:S(2)}) collective-permute-start(bf16[512,512]{1,0:T(8,128)(2,1)S(1)} %and_select_fusion.1), channel_id=1, source_target_pairs={{0,8},{8,16},{16,24},{24,32},{32,40},{40,48},{48,56},{56,64},{64,7... | collective-permute-start | bytes 1572872 | tf_op jit(solution)/shard_map/ppermute | solution.py:12
  12.5 90.7 %collective-permute-start.1 = (bf16[512,512]{1,0:T(8,128)(2,1)S(1)}, bf16[512,512]{1,0:T(8,128)(2,1)S(1)}, u32[]{:S(2)}, u32[]{:S(2)}) collective-permute-start(bf16[512,512]{1,0:T(8,128)(2,1)S(1)} %and_select_fusion.1), channel_id=1, source_target_pairs={{8,0},{16,8},{24,16},{32,24},{40,32},{48,40},{56,48},{64,56},{72,6... | collective-permute-start | bytes 1572872 | tf_op jit(solution)/shard_map/ppermute | solution.py:12
  21.9 88.1 %collective-permute-start.2 = (bf16[512,512]{1,0:T(8,128)(2,1)S(1)}, bf16[512,512]{1,0:T(8,128)(2,1)S(1)}, u32[]{:S(2)}, u32[]{:S(2)}) collective-permute-start(bf16[512,512]{1,0:T(8,128)(2,1)S(1)} %and_select_fusion.1), channel_id=1, source_target_pairs={{0,64},{8,72},{16,80},{24,88},{32,96},{40,104},{48,112},{56,120},{... | collective-permute-start | bytes 1572872 | tf_op jit(solution)/shard_map/ppermute | solution.py:12
  31.4 95.4 %collective-permute-start.3 = (bf16[512,512]{1,0:T(8,128)(2,1)S(1)}, bf16[512,512]{1,0:T(8,128)(2,1)S(1)}, u32[]{:S(2)}, u32[]{:S(2)}) collective-permute-start(bf16[512,512]{1,0:T(8,128)(2,1)S(1)} %and_select_fusion.1), channel_id=1, source_target_pairs={{64,0},{72,8},{80,16},{88,24},{96,32},{104,40},{112,48},{120,56},{... | collective-permute-start | bytes 1572872 | tf_op jit(solution)/shard_map/ppermute | solution.py:12
  131.4 3.1 %copy-start.1 = (bf16[4,1,512,512]{3,2,1,0:T(8,128)(2,1)S(1)}, bf16[4,1,512,512]{3,2,1,0:T(8,128)(2,1)}, u32[]{:S(2)}) copy-start(bf16[4,1,512,512]{3,2,1,0:T(8,128)(2,1)} %param.8) | copy-start | bytes 6291460
  131.4 3.1 %copy-start.2 = (f32[4]{0:T(128)S(1)}, f32[4]{0:T(128)}, u32[]{:S(2)}) copy-start(f32[4]{0:T(128)} %param.10) | copy-start | bytes 52
Sparse Core Ops, SparseCore 0:
  139.9 75.1 all-reduce.1
where the time goes:
time: 224 us
  waiting for transfers between devices  159 us (71%)
  starting transfers between devices  28.8 us (13%)
  between operations  14.3 us (6%)
  local copies, waits for them, and re-layouts  8.64 us (4%)
  matrix products  7.07 us (3%)
  other arithmetic  5.84 us (3%)
    ppermute x4, waiting for transfers between devices, shifted(): return lax.ppermute(block, axis, route)  83.6 us
    psum x1, waiting for transfers between devices, per_device(): lax.psum(jnp.where(block_mask, weighted, jnp.zeros_like(weighted)), 'mpo')  75.4 us
    ppermute x4, starting transfers between devices, shifted(): return lax.ppermute(block, axis, route)  28.8 us
  transfers between devices with their start and end apart: 5, of which 4 were waited for; matrix products, arithmetic and copies ran while one was open for 3% of the time, Pallas kernels for 0%

commit v1 on v0

v1 whole, which is shorter than its diff:
```python
import functools

import jax
import jax.numpy as jnp
from jax import lax
from jax.experimental import pallas as pl
from jax.experimental.pallas import tpu as pltpu
from jax.sharding import PartitionSpec as P


GRID = 8
CORES = 2
NEAR = ((2.0, 1.0), (1.0, 2.0))
FAR = ((4.0, 3.0), (3.0, 4.0))


def terms_kernel(early, size, parity, mine, other, *rest):
    lefts, rights, rest = rest[0:2], rest[2:4], rest[4:]
    n = 3 if early else 2
    sources, rest = rest[:n], rest[n:]
    if not early:
        before, rest = rest[0], rest[1:]
    out, left_buf, right_buf, acc, left_sem, right_sem = rest
    count, chips, step, extent = left_buf.shape[0] // 2, *left_buf.shape[1:]
    core = parity[0]

    def code(w):
        return jnp.where(w < count, mine[w % count], other[w % count])

    def uses(w, source):
        if early and source == 0:
            return code(w) == 0.0
        table = (NEAR if early else FAR)[source - 1 if early else source]
        return code(w) == jnp.where(core == 0, table[0], table[1])

    def fetch_left(w, k):
        return pltpu.make_async_copy(lefts[k].at[w % count, :, core], left_buf.at[w], left_sem.at[w])

    def fetch_right(w, k):
        return pltpu.make_async_copy(rights[k].at[w % count], right_buf.at[w], right_sem.at[w])

    for k in range(n):
        for w in range(2 * count):
            @pl.when(uses(w, k))
            def _():
                fetch_left(w, w // count).start()
                fetch_right(w, w // count).start()

    if early:
        acc[...] = jnp.zeros_like(acc)
    else:
        acc[...] = before[...]

    for k in range(n):
        @pl.loop(0, 2 * count)
        def _(w):
            @pl.when(uses(w, k))
            def _():
                fetch_left(w, 0).wait()
                product = jnp.dot(
                    left_buf[w].reshape(chips * step, extent),
                    sources[k][...],
                    preferred_element_type=jnp.float32,
                )
                scale = jnp.where(w < count, mine[count + w % count], other[count + w % count])
                product = product * scale
                high = product.astype(jnp.bfloat16)
                low = (product - high.astype(jnp.float32)).astype(jnp.bfloat16)
                fetch_right(w, 0).wait()
                along = (((1,), (1,)), ((), ()))
                total = lax.dot_general(
                    high, right_buf[w], along, preferred_element_type=jnp.float32
                )
                total += lax.dot_general(
                    low, right_buf[w], along, preferred_element_type=jnp.float32
                )
                acc[...] += total

    if early:
        out[...] = acc[...]
        return
    for y in range(chips):
        row = (y * CORES + core) * step + lax.broadcasted_iota(jnp.int32, (step, extent), 0)
        column = lax.broadcasted_iota(jnp.int32, (step, extent), 1)
        live = (row < size[0]) & (column < size[0])
        out[y] = jnp.where(live, acc[pl.ds(y * step, step), :], 0.0)


def terms(sources, before, size, parity, mine, other, lefts, rights):
    early = before is None
    count, chips, _, step, extent = lefts[0].shape
    smem = pl.BlockSpec(memory_space=pltpu.SMEM)
    vmem = pl.BlockSpec(memory_space=pltpu.VMEM)
    anywhere = pl.BlockSpec(memory_space=pl.ANY)
    shape = (chips * step, extent) if early else (chips, step, extent)
    held = sources if early else (*sources, before)
    held = [pltpu.with_memory_space_constraint(a, pltpu.VMEM) for a in held]
    return pl.pallas_call(
        functools.partial(terms_kernel, early),
        out_shape=jax.ShapeDtypeStruct(shape, jnp.float32),
        in_specs=[smem] * 4 + [anywhere] * 4 + [vmem] * len(held),
        out_specs=vmem,
        scratch_shapes=[
            pltpu.VMEM((2 * count, chips, step, extent), jnp.bfloat16),
            pltpu.VMEM((2 * count, extent, extent), jnp.bfloat16),
            pltpu.VMEM((chips * step, extent), jnp.float32),
            pltpu.SemaphoreType.DMA((2 * count,)),
            pltpu.SemaphoreType.DMA((2 * count,)),
        ],
        compiler_params=pltpu.CompilerParams(vmem_limit_bytes=16 << 20),
        cost_estimate=pl.CostEstimate(
            flops=count * extent**3 * 3, bytes_accessed=count * extent**2 * 4, transcendentals=0
        ),
    )(size, parity, mine, other, *lefts, *rights, *held)


def per_device(
    wavefunction, left_environment, right_environment, term_shift, coupling, block_sizes
):
    extent = wavefunction.shape[1]
    sectors, members = lax.axis_size("sector"), lax.axis_size("mpo")
    chips = members // CORES
    step = extent // members
    me = lax.axis_index("mpo")
    chip, parity = me // CORES, me % CORES
    both = ("sector", "mpo")
    same_core = [[y * CORES + c for y in range(chips)] for c in range(CORES)]
    swap = [(m, m ^ 1) for m in range(members)]

    def route(source_of):
        pairs = []
        for s in range(sectors):
            for m in range(members):
                source, core = source_of(s, m % CORES)
                if 0 <= source < sectors:
                    pairs.append((source * members + m - m % CORES + core, s * members + m))
        return pairs

    late = lambda s: s % (2 * GRID) >= GRID
    nowhere = (-1, 0)
    near = route(lambda s, c: (s + 1, 0) if c == 0 else (s - 1, 1))
    far_above = route(lambda s, c: (s + GRID, 0) if c == 0 else nowhere)
    far_below = route(
        lambda s, c: nowhere if c == 0 else (s - GRID, 0 if late(s - GRID) else 1)
    )

    size = block_sizes[0]
    positions = jnp.arange(extent)
    share = extent // chips
    strip = lax.dynamic_slice_in_dim(wavefunction[0], chip * share, share, 0)
    rows = chip * share + jnp.arange(share)
    strip = jnp.where((rows < size)[:, None] & (positions < size)[None, :], strip, 0)
    above_strip = lax.ppermute(strip, both, far_above)
    below_strip = lax.ppermute(strip, both, far_below)
    live = positions < size
    masked = jnp.where(live[:, None] & live[None, :], wavefunction[0], 0)
    near_one = lax.ppermute(masked, both, near)

    in_hbm = lambda a: pltpu.with_memory_space_constraint(a, pltpu.HBM)
    by_core = lambda a: in_hbm(a.reshape(a.shape[0], chips, CORES, step, extent))
    left, right = left_environment[:, 0], right_environment[:, 0]
    mine = jnp.concatenate([term_shift.astype(jnp.float32), coupling])
    right_other = lax.ppermute(right, "mpo", swap)
    left_other = lax.ppermute(left, "mpo", swap)
    other = lax.ppermute(mine, "mpo", swap)
    near_two = lax.ppermute(near_one, "mpo", swap)
    lefts = (by_core(left), by_core(left_other))
    rights = (in_hbm(right), in_hbm(right_other))
    shared = (block_sizes, parity[None].astype(jnp.int32), mine, other, lefts, rights)

    far_strip = jnp.where(parity == 0, above_strip, below_strip)
    spread = jnp.broadcast_to(far_strip[None], (chips,) + far_strip.shape)
    far_one = lax.all_to_all(spread, "mpo", 0, 0, axis_index_groups=same_core)
    far_one = far_one.reshape(extent, extent)
    early = terms((masked, near_one, near_two), None, *shared)
    far_two = lax.ppermute(far_one, "mpo", swap)
    half = terms((far_one, far_two), early, *shared)
    pieces = lax.all_to_all(half, "mpo", 0, 0, axis_index_groups=same_core)
    return jnp.sum(pieces, axis=0)[None]


def solution(mesh):
    placed = (
        P("sector", None, None),
        P("mpo", "sector", None, None),
        P("mpo", "sector", None, None),
        P("mpo"),
        P("mpo"),
        P("sector"),
    )

    return jax.shard_map(
        per_device, mesh=mesh, in_specs=placed, out_specs=P("sector", "mpo", None), check_vma=False
    )
```

time: 224 us -> 78.3 us (0.35)
  the two profiles are of different devices: /device:TPU:2 before, /device:TPU:38 now
where the time goes in v1:
time: 78.3 us; the launch traced here: 77.8 us
  starting transfers between devices  34.3 us (44%)
  waiting for transfers between devices  16 us (20%)
  blocking collectives  12.5 us (16%)
  Pallas kernels  10.3 us (13%)
  other arithmetic  3.08 us (4%)
  local copies, waits for them, and re-layouts  0.86 us (1%)
  between operations  0.83 us (1%)
    ppermute x1, starting transfers between devices, per_device(): above_strip = lax.ppermute(strip, both, far_above)  15.1 us
    all_to_all x1, blocking collectives, per_device(): pieces = lax.all_to_all(half, 'mpo', 0, 0, axis_index_groups=same_core)  12.5 us
    pallas_call x2, Pallas kernels, terms(): pl.pallas_call(functools.partial(terms_kernel, early), out_shape=jax.Shap...  10.3 us
    all_to_all x1, waiting for transfers between devices, per_device(): far_one = lax.all_to_all(spread, 'mpo', 0, 0, axis_index_groups=same_core)  8.01 us
    ppermute x1, waiting for transfers between devices, per_device(): above_strip = lax.ppermute(strip, both, far_above)  6.91 us
    all_to_all x1, starting transfers between devices, per_device(): far_one = lax.all_to_all(spread, 'mpo', 0, 0, axis_index_groups=same_core)  4.46 us
    ppermute x1, starting transfers between devices, per_device(): near_one = lax.ppermute(masked, both, near)  2.92 us
    ppermute x1, starting transfers between devices, per_device(): near_two = lax.ppermute(near_one, 'mpo', swap)  2.42 us
  transfers between devices with their start and end apart: 9, of which 4 were waited for; matrix products, arithmetic and copies ran while one was open for 4% of the time, Pallas kernels for 9%

profile of v1, /device:TPU:38, one launch (start us, length us, event | category | flops | bytes accessed | tf_op | source)
XLA Modules:
  0.0 77.8 jit_solution(17123855365334145546)
XLA Ops:
  0.0 2.0 %collective-permute-start.2 = (bf16[4,512,512]{2,1,0:T(8,128)(2,1)}, bf16[4,512,512]{2,1,0:T(8,128)(2,1)}, u32[]{:S(2)}, u32[]{:S(2)}) collective-permute-start(bf16[4,512,512]{2,1,0:T(8,128)(2,1)} %bitcast.19), channel_id=1, source_target_pairs={{0,1},{1,0},{2,3},{3,2},{4,5},{5,4},{6,7},{7,6},{8,9},{9,8},{10,11... | collective-permute-start | bytes 6291464 | tf_op jit(solution)/shard_map/ppermute | solution.py:163
  2.1 2.4 %collective-permute-start.1 = (bf16[4,512,512]{2,1,0:T(8,128)(2,1)}, bf16[4,512,512]{2,1,0:T(8,128)(2,1)}, u32[]{:S(2)}, u32[]{:S(2)}) collective-permute-start(bf16[4,512,512]{2,1,0:T(8,128)(2,1)} %bitcast.16), channel_id=1, source_target_pairs={{0,1},{1,0},{2,3},{3,2},{4,5},{5,4},{6,7},{7,6},{8,9},{9,8},{10,11... | collective-permute-start | bytes 6291464 | tf_op jit(solution)/shard_map/ppermute | solution.py:164
  5.2 1.0 %and_select_fusion.1 = bf16[128,512]{1,0:T(8,128)(2,1)S(1)} fusion(bf16[1,512,512]{2,1,0:T(8,128)(2,1)} %param.6, s32[]{:T(128)S(6)} %select_n.33, pred[512]{0:T(512)(128)(4,1)S(1)} %iota_compare_fusion, pred[128]{0:T(512)(128)(4,1)S(1)} %add_compare_fusion), kind=kLoop, calls=%fused_computation.1 | loop fusion | flops 131072 | bytes 262788 | tf_op jit(solution)/shard_map/jit(_where)/select_n | solution.py:152
  6.2 15.1 %collective-permute-start.3 = (bf16[128,512]{1,0:T(8,128)(2,1)S(1)}, bf16[128,512]{1,0:T(8,128)(2,1)S(1)}, u32[]{:S(2)}, u32[]{:S(2)}) collective-permute-start(bf16[128,512]{1,0:T(8,128)(2,1)S(1)} %and_select_fusion.1), channel_id=1, source_target_pairs={{64,0},{66,2},{68,4},{70,6},{72,8},{74,10},{76,12},{78,14},{80,16}... | collective-permute-start | bytes 393224 | tf_op jit(solution)/shard_map/ppermute | solution.py:153
  21.3 0.7 collective-permute-start.4
  22.0 1.3 %and_select_fusion.rest_4_ = bf16[512,512]{1,0:T(8,128)(2,1)S(1)} fusion(bf16[1,512,512]{2,1,0:T(8,128)(2,1)} %param.6, pred[512]{0:T(512)(128)(4,1)S(1)} %iota_compare_fusion), kind=kLoop, calls=%fused_computation | loop fusion | flops 524288 | bytes 1049088 | tf_op jit(solution)/shard_map/jit(_where)/select_n | solution.py:156
  23.2 2.9 %collective-permute-start.6 = (bf16[512,512]{1,0:T(8,128)(2,1)S(1)}, bf16[512,512]{1,0:T(8,128)(2,1)S(1)}, u32[]{:S(2)}, u32[]{:S(2)}) collective-permute-start(bf16[512,512]{1,0:T(8,128)(2,1)S(1)} %and_select_fusion.rest_4_), channel_id=1, source_target_pairs={{8,0},{10,2},{12,4},{14,6},{16,8},{1,9},{18,10},{3,11},{20,12},{5,... | collective-permute-start | bytes 1572872 | tf_op jit(solution)/shard_map/ppermute | solution.py:157
  26.2 6.9 %collective-permute-done.3 = bf16[128,512]{1,0:T(8,128)(2,1)S(1)} collective-permute-done((bf16[128,512]{1,0:T(8,128)(2,1)S(1)}, bf16[128,512]{1,0:T(8,128)(2,1)S(1)}, u32[]{:S(2)}, u32[]{:S(2)}) %collective-permute-start.3) | collective-permute-done | bytes 131104 | tf_op jit(solution)/shard_map/ppermute | solution.py:153
  33.1 0.0 collective-permute-done.4
  33.1 0.8 %broadcast_in_dim.26 = bf16[4,128,512]{2,1,0:T(8,128)(2,1)} broadcast(bf16[128,512]{1,0:T(8,128)(2,1)S(1)} %broadcast_select_fusion), dimensions={1,2} | broadcast | bytes 655360 | tf_op jit(solution)/shard_map/broadcast_in_dim | solution.py:172
  33.9 4.5 %all-to-all-start = ((bf16[4,128,512]{2,1,0:T(8,128)(2,1)}), bf16[4,128,512]{2,1,0:T(8,128)(2,1)S(1)}, u32[]{:S(2)}, u32[]{:S(2)}) async-start(bf16[4,128,512]{2,1,0:T(8,128)(2,1)} %broadcast_in_dim.26), calls=%async_computation | async-start | bytes 1048576 | tf_op jit(solution)/shard_map/all_to_all | solution.py:173
  38.4 0.3 collective-permute-done.6.rest_5_
  38.7 2.4 %collective-permute-start.7 = (bf16[512,512]{1,0:T(8,128)(2,1)S(1)}, bf16[512,512]{1,0:T(8,128)(2,1)S(1)}, u32[]{:S(2)}, u32[]{:S(2)}) collective-permute-start(bf16[512,512]{1,0:T(8,128)(2,1)S(1)} %collective-permute-done.6.rest_5_), channel_id=1, source_target_pairs={{0,1},{1,0},{2,3},{3,2},{4,5},{5,4},{6,7},{7,6},{8,9},{9,8},{10,11... | collective-permute-start | bytes 1572872 | tf_op jit(solution)/shard_map/ppermute | solution.py:166
  41.1 8.0 %all-to-all-done = bf16[4,128,512]{2,1,0:T(8,128)(2,1)S(1)} async-done(((bf16[4,128,512]{2,1,0:T(8,128)(2,1)}), bf16[4,128,512]{2,1,0:T(8,128)(2,1)S(1)}, u32[]{:S(2)}, u32[]{:S(2)}) %all-to-all-start) | async-done | bytes 524320 | tf_op jit(solution)/shard_map/all_to_all | solution.py:173
  49.1 1.9 %collective-permute-start.5 = (bf16[512,512]{1,0:T(8,128)(2,1)S(1)}, bf16[512,512]{1,0:T(8,128)(2,1)S(1)}, u32[]{:S(2)}, u32[]{:S(2)}) collective-permute-start(bf16[512,512]{1,0:T(8,128)(2,1)S(1)} %bitcast.14), channel_id=1, source_target_pairs={{0,1},{1,0},{2,3},{3,2},{4,5},{5,4},{6,7},{7,6},{8,9},{9,8},{10,11... | collective-permute-start | bytes 1572872 | tf_op jit(solution)/shard_map/ppermute | solution.py:176
  51.1 0.1 pad_maximum_fusion.mine
  51.2 2.4 %collective-permute-start = (f32[8]{0:T(128)S(1)}, f32[8]{0:T(128)S(1)}, u32[]{:S(2)}, u32[]{:S(2)}) collective-permute-start(f32[8]{0:T(128)S(1)} %pad_maximum_fusion.mine), channel_id=1, source_target_pairs={{0,1},{1,0},{2,3},{3,2},{4,5},{5,4},{6,7},{7,6},{8,9},{9,8},{10,11... | collective-permute-start | bytes 104 | tf_op jit(solution)/shard_map/ppermute | solution.py:165
  53.6 0.8 %collective-permute-done.other = f32[8]{0:T(128)S(1)} collective-permute-done((f32[8]{0:T(128)S(1)}, f32[8]{0:T(128)S(1)}, u32[]{:S(2)}, u32[]{:S(2)}) %collective-permute-start) | collective-permute-done | bytes 64 | tf_op jit(solution)/shard_map/ppermute | solution.py:165
  54.4 0.0 collective-permute-done.7.rest_6_
  54.4 6.7 %shard_map.64.rest_6_ = f32[256,512]{1,0:T(8,128)S(1)} custom-call(s32[1]{0:T(128)} %copy.7.size, s32[1]{0:T(128)} %bitcast.parity, f32[8]{0:T(128)S(1)} %pad_maximum_fusion.mine, f32[8]{0:T(128)S(1)} %collective-permute-done.other, bf16[4,4,2,64,512]{4,3,2,1,0:T(8,128)(2,1)} %bitcast.17, bf16[4,4,2,64,512]{4,3,2,1,0:T(8,128)(2,1)} %bitcast.3.rest_1_, ...), custom_call_target="tpu_custom_call" | custom-call | flops 1610612736 | bytes 4194304 | tf_op jit(solution)/shard_map/pallas_call | solution.py:98
  61.1 0.0 collective-permute-done.5.rest_5_
  61.1 3.5 %shard_map.65 = f32[4,64,512]{2,1,0:T(8,128)S(1)} custom-call(s32[1]{0:T(128)} %copy.7.size, s32[1]{0:T(128)} %bitcast.parity, f32[8]{0:T(128)S(1)} %pad_maximum_fusion.mine, f32[8]{0:T(128)S(1)} %collective-permute-done.other, bf16[4,4,2,64,512]{4,3,2,1,0:T(8,128)(2,1)} %bitcast.18, bf16[4,4,2,64,512]{4,3,2,1,0:T(8,128)(2,1)} %bitcast.3.rest_1_, ...), custom_call_target="tpu_custom_call" | custom-call | flops 1610612736 | bytes 4194304 | tf_op jit(solution)/shard_map/pallas_call | solution.py:98
  64.7 12.5 %all_to_all.10 = f32[4,64,512]{2,1,0:T(8,128)S(1)} all-to-all(f32[4,64,512]{2,1,0:T(8,128)S(1)} %shard_map.65), channel_id=1, replica_groups={{0,2,4,6},{1,3,5,7},{8,10,12,14},{9,11,13,15},{16,18,20,22},{17,19,21,2..., dimensions={0} | all-to-all | bytes 1048576 | tf_op jit(solution)/shard_map/all_to_all | solution.py:178
  77.1 0.7 reduce_sum.9
  (10 shorter events, 0.0 us)
Async XLA Ops:
  0.0 51.1 %copy-start = (s32[4]{0:T(128)S(1)}, s32[4]{0:T(128)}, u32[]{:S(2)}) copy-start(s32[4]{0:T(128)} %param.9) | copy-start | bytes 52
  0.0 51.1 %copy-start.1 = (f32[4]{0:T(128)S(1)}, f32[4]{0:T(128)}, u32[]{:S(2)}) copy-start(f32[4]{0:T(128)} %param.10) | copy-start | bytes 52
  0.0 54.4 %collective-permute-start.2 = (bf16[4,512,512]{2,1,0:T(8,128)(2,1)}, bf16[4,512,512]{2,1,0:T(8,128)(2,1)}, u32[]{:S(2)}, u32[]{:S(2)}) collective-permute-start(bf16[4,512,512]{2,1,0:T(8,128)(2,1)} %bitcast.19), channel_id=1, source_target_pairs={{0,1},{1,0},{2,3},{3,2},{4,5},{5,4},{6,7},{7,6},{8,9},{9,8},{10,11... | collective-permute-start | bytes 6291464 | tf_op jit(solution)/shard_map/ppermute | solution.py:163
  2.1 52.3 %collective-permute-start.1 = (bf16[4,512,512]{2,1,0:T(8,128)(2,1)}, bf16[4,512,512]{2,1,0:T(8,128)(2,1)}, u32[]{:S(2)}, u32[]{:S(2)}) collective-permute-start(bf16[4,512,512]{2,1,0:T(8,128)(2,1)} %bitcast.16), channel_id=1, source_target_pairs={{0,1},{1,0},{2,3},{3,2},{4,5},{5,4},{6,7},{7,6},{8,9},{9,8},{10,11... | collective-permute-start | bytes 6291464 | tf_op jit(solution)/shard_map/ppermute | solution.py:164
  6.2 26.9 %collective-permute-start.3 = (bf16[128,512]{1,0:T(8,128)(2,1)S(1)}, bf16[128,512]{1,0:T(8,128)(2,1)S(1)}, u32[]{:S(2)}, u32[]{:S(2)}) collective-permute-start(bf16[128,512]{1,0:T(8,128)(2,1)S(1)} %and_select_fusion.1), channel_id=1, source_target_pairs={{64,0},{66,2},{68,4},{70,6},{72,8},{74,10},{76,12},{78,14},{80,16}... | collective-permute-start | bytes 393224 | tf_op jit(solution)/shard_map/ppermute | solution.py:153
  21.3 11.8 %collective-permute-start.4 = (bf16[128,512]{1,0:T(8,128)(2,1)S(1)}, bf16[128,512]{1,0:T(8,128)(2,1)S(1)}, u32[]{:S(2)}, u32[]{:S(2)}) collective-permute-start(bf16[128,512]{1,0:T(8,128)(2,1)S(1)} %and_select_fusion.1), channel_id=1, source_target_pairs={{1,65},{3,67},{5,69},{7,71},{9,73},{11,75},{13,77},{15,79},{17,81}... | collective-permute-start | bytes 393224 | tf_op jit(solution)/shard_map/ppermute | solution.py:154
  23.2 15.5 %collective-permute-start.6 = (bf16[512,512]{1,0:T(8,128)(2,1)S(1)}, bf16[512,512]{1,0:T(8,128)(2,1)S(1)}, u32[]{:S(2)}, u32[]{:S(2)}) collective-permute-start(bf16[512,512]{1,0:T(8,128)(2,1)S(1)} %and_select_fusion.rest_4_), channel_id=1, source_target_pairs={{8,0},{10,2},{12,4},{14,6},{16,8},{1,9},{18,10},{3,11},{20,12},{5,... | collective-permute-start | bytes 1572872 | tf_op jit(solution)/shard_map/ppermute | solution.py:157
  33.9 15.2 %all-to-all-start = ((bf16[4,128,512]{2,1,0:T(8,128)(2,1)}), bf16[4,128,512]{2,1,0:T(8,128)(2,1)S(1)}, u32[]{:S(2)}, u32[]{:S(2)}) async-start(bf16[4,128,512]{2,1,0:T(8,128)(2,1)} %broadcast_in_dim.26), calls=%async_computation | async-start | bytes 1048576 | tf_op jit(solution)/shard_map/all_to_all | solution.py:173
  38.7 15.7 %collective-permute-start.7 = (bf16[512,512]{1,0:T(8,128)(2,1)S(1)}, bf16[512,512]{1,0:T(8,128)(2,1)S(1)}, u32[]{:S(2)}, u32[]{:S(2)}) collective-permute-start(bf16[512,512]{1,0:T(8,128)(2,1)S(1)} %collective-permute-done.6.rest_5_), channel_id=1, source_target_pairs={{0,1},{1,0},{2,3},{3,2},{4,5},{5,4},{6,7},{7,6},{8,9},{9,8},{10,11... | collective-permute-start | bytes 1572872 | tf_op jit(solution)/shard_map/ppermute | solution.py:166
  49.1 12.0 %collective-permute-start.5 = (bf16[512,512]{1,0:T(8,128)(2,1)S(1)}, bf16[512,512]{1,0:T(8,128)(2,1)S(1)}, u32[]{:S(2)}, u32[]{:S(2)}) collective-permute-start(bf16[512,512]{1,0:T(8,128)(2,1)S(1)} %bitcast.14), channel_id=1, source_target_pairs={{0,1},{1,0},{2,3},{3,2},{4,5},{5,4},{6,7},{7,6},{8,9},{9,8},{10,11... | collective-permute-start | bytes 1572872 | tf_op jit(solution)/shard_map/ppermute | solution.py:176
  51.2 3.2 %collective-permute-start = (f32[8]{0:T(128)S(1)}, f32[8]{0:T(128)S(1)}, u32[]{:S(2)}, u32[]{:S(2)}) collective-permute-start(f32[8]{0:T(128)S(1)} %pad_maximum_fusion.mine), channel_id=1, source_target_pairs={{0,1},{1,0},{2,3},{3,2},{4,5},{5,4},{6,7},{7,6},{8,9},{9,8},{10,11... | collective-permute-start | bytes 104 | tf_op jit(solution)/shard_map/ppermute | solution.py:165

commit v2 on v1

--- a/solution.py
+++ b/solution.py
@@ -10,71 +10,75 @@
 
 GRID = 8
 CORES = 2
-NEAR = ((2.0, 1.0), (1.0, 2.0))
-FAR = ((4.0, 3.0), (3.0, 4.0))
+EARLY = ((0.0, 0.0), (2.0, 1.0), (1.0, 2.0))
+LATE = ((4.0, 3.0), (3.0, 4.0))
 
 
 def terms_kernel(early, size, parity, mine, other, *rest):
     lefts, rights, rest = rest[0:2], rest[2:4], rest[4:]
-    n = 3 if early else 2
+    codes = EARLY if early else LATE
+    n = len(codes)
     sources, rest = rest[:n], rest[n:]
     if not early:
         before, rest = rest[0], rest[1:]
-    out, left_buf, right_buf, acc, left_sem, right_sem = rest
-    count, chips, step, extent = left_buf.shape[0] // 2, *left_buf.shape[1:]
+    out, left_buf, right_buf, acc, scale, sems = rest
+    count, (chips, step, extent) = left_buf.shape[0] // 2, left_buf.shape[1:]
     core = parity[0]
 
-    def code(w):
-        return jnp.where(w < count, mine[w % count], other[w % count])
-
-    def uses(w, source):
-        if early and source == 0:
-            return code(w) == 0.0
-        table = (NEAR if early else FAR)[source - 1 if early else source]
-        return code(w) == jnp.where(core == 0, table[0], table[1])
-
-    def fetch_left(w, k):
-        return pltpu.make_async_copy(lefts[k].at[w % count, :, core], left_buf.at[w], left_sem.at[w])
-
-    def fetch_right(w, k):
-        return pltpu.make_async_copy(rights[k].at[w % count], right_buf.at[w], right_sem.at[w])
-
-    for k in range(n):
-        for w in range(2 * count):
-            @pl.when(uses(w, k))
-            def _():
-                fetch_left(w, w // count).start()
-                fetch_right(w, w // count).start()
+    def fetch_left(k, w, at):
+        return pltpu.make_async_copy(lefts[k].at[w, :, core], left_buf.at[at], sems.at[0, at])
+
+    def fetch_right(k, w, at):
+        return pltpu.make_async_copy(rights[k].at[w], right_buf.at[at], sems.at[1, at])
+
+    found, begins = jnp.int32(0), []
+    for on_core in codes:
+        begins.append(found)
+        for k, facts in enumerate((mine, other)):
+            for w in range(count):
+                takes = facts[w] == jnp.where(core == 0, *on_core)
+
+                @pl.when(takes)
+                def _(found=found):
+                    fetch_left(k, w, found).start()
+                    fetch_right(k, w, found).start()
+                    scale[found] = facts[count + w]
+
+                found += takes.astype(jnp.int32)
+    begins.append(found)
 
     if early:
         acc[...] = jnp.zeros_like(acc)
     else:
         acc[...] = before[...]
 
-    for k in range(n):
-        @pl.loop(0, 2 * count)
-        def _(w):
-            @pl.when(uses(w, k))
-            def _():
-                fetch_left(w, 0).wait()
-                product = jnp.dot(
-                    left_buf[w].reshape(chips * step, extent),
-                    sources[k][...],
-                    preferred_element_type=jnp.float32,
-                )
-                scale = jnp.where(w < count, mine[count + w % count], other[count + w % count])
-                product = product * scale
-                high = product.astype(jnp.bfloat16)
-                low = (product - high.astype(jnp.float32)).astype(jnp.bfloat16)
-                fetch_right(w, 0).wait()
-                along = (((1,), (1,)), ((), ()))
-                total = lax.dot_general(
-                    high, right_buf[w], along, preferred_element_type=jnp.float32
-                )
-                total += lax.dot_general(
-                    low, right_buf[w], along, preferred_element_type=jnp.float32
-                )
-                acc[...] += total
+    along = (((1,), (1,)), ((), ()))
+
+    def add(source, slots):
+        parts = []
+        for at in slots:
+            fetch_left(0, 0, at).wait()
+            rows = left_buf[at].reshape(chips * step, extent)
+            product = jnp.dot(rows, source[...], preferred_element_type=jnp.float32) * scale[at]
+            high = product.astype(jnp.bfloat16)
+            low = (product - high.astype(jnp.float32)).astype(jnp.bfloat16)
+            parts.append((high, low))
+        total = acc[...]
+        for at, (high, low) in zip(slots, parts):
+            fetch_right(0, 0, at).wait()
+            right = right_buf[at]
+            total += lax.dot_general(high, right, along, preferred_element_type=jnp.float32)
+            total += lax.dot_general(low, right, along, preferred_element_type=jnp.float32)
+        acc[...] = total
+
+    for source, begin, end in zip(sources, begins, begins[1:]):
+        @pl.loop(0, (end - begin) >> 1)
+        def _(pair):
+            add(source, (begin + 2 * pair, begin + 2 * pair + 1))
+
+        @pl.when(((end - begin) & 1) == 1)
+        def _():
+            add(source, (end - 1,))
 
     if early:
         out[...] = acc[...]
@@ -104,8 +108,8 @@
             pltpu.VMEM((2 * count, chips, step, extent), jnp.bfloat16),
             pltpu.VMEM((2 * count, extent, extent), jnp.bfloat16),
             pltpu.VMEM((chips * step, extent), jnp.float32),
-            pltpu.SemaphoreType.DMA((2 * count,)),
-            pltpu.SemaphoreType.DMA((2 * count,)),
+            pltpu.SMEM((2 * count,), jnp.float32),
+            pltpu.SemaphoreType.DMA((2, 2 * count)),
         ],
         compiler_params=pltpu.CompilerParams(vmem_limit_bytes=16 << 20),
         cost_estimate=pl.CostEstimate(
@@ -159,7 +163,12 @@
     in_hbm = lambda a: pltpu.with_memory_space_constraint(a, pltpu.HBM)
     by_core = lambda a: in_hbm(a.reshape(a.shape[0], chips, CORES, step, extent))
     left, right = left_environment[:, 0], right_environment[:, 0]
-    mine = jnp.concatenate([term_shift.astype(jnp.float32), coupling])
+    count = coupling.shape[0]
+    mine = jnp.where(
+        jnp.arange(2 * count) < count,
+        jnp.pad(term_shift, (0, count)).astype(jnp.float32),
+        jnp.pad(coupling, (count, 0)),
+    )
     right_other = lax.ppermute(right, "mpo", swap)
     left_other = lax.ppermute(left, "mpo", swap)
     other = lax.ppermute(mine, "mpo", swap)

time: 78.3 us -> 77.7 us (level)
  Pallas kernels: 10.3 us -> 9.49 us
  transfers between devices with their start and end apart: 9 -> 9, of which waited for: 4 -> 4; matrix products, arithmetic and copies ran while one was open for 4% -> 4% of each run, Pallas kernels for 9% -> 8%
where the time goes in v2:
time: 77.7 us; the launch traced here: 77.3 us
  starting transfers between devices  34.3 us (44%)
  waiting for transfers between devices  16 us (21%)
  blocking collectives  12.7 us (16%)
  Pallas kernels  9.49 us (12%)
  other arithmetic  3.07 us (4%)
  local copies, waits for them, and re-layouts  0.86 us (1%)
  between operations  0.82 us (1%)
    ppermute x1, starting transfers between devices, per_device(): above_strip = lax.ppermute(strip, both, far_above)  15.1 us
    all_to_all x1, blocking collectives, per_device(): pieces = lax.all_to_all(half, 'mpo', 0, 0, axis_index_groups=same_core)  12.7 us
    pallas_call x2, Pallas kernels, terms(): pl.pallas_call(functools.partial(terms_kernel, early), out_shape=jax.Shap...  9.49 us
    all_to_all x1, waiting for transfers between devices, per_device(): far_one = lax.all_to_all(spread, 'mpo', 0, 0, axis_index_groups=same_core)  8.01 us
    ppermute x1, waiting for transfers between devices, per_device(): above_strip = lax.ppermute(strip, both, far_above)  6.91 us
    all_to_all x1, starting transfers between devices, per_device(): far_one = lax.all_to_all(spread, 'mpo', 0, 0, axis_index_groups=same_core)  4.46 us
    ppermute x1, starting transfers between devices, per_device(): near_one = lax.ppermute(masked, both, near)  2.92 us
    ppermute x1, starting transfers between devices, per_device(): near_two = lax.ppermute(near_one, 'mpo', swap)  2.42 us
  transfers between devices with their start and end apart: 9, of which 4 were waited for; matrix products, arithmetic and copies ran while one was open for 4% of the time, Pallas kernels for 8%

profile of v2, /device:TPU:38, one launch (start us, length us, event | category | flops | bytes accessed | tf_op | source)
XLA Modules:
  0.0 77.3 jit_solution(6456944522811081984)
XLA Ops:
  0.0 2.0 %collective-permute-start.2 = (bf16[4,512,512]{2,1,0:T(8,128)(2,1)}, bf16[4,512,512]{2,1,0:T(8,128)(2,1)}, u32[]{:S(2)}, u32[]{:S(2)}) collective-permute-start(bf16[4,512,512]{2,1,0:T(8,128)(2,1)} %bitcast.19), channel_id=1, source_target_pairs={{0,1},{1,0},{2,3},{3,2},{4,5},{5,4},{6,7},{7,6},{8,9},{9,8},{10,11... | collective-permute-start | bytes 6291464 | tf_op jit(solution)/shard_map/ppermute | solution.py:172
  2.1 2.4 %collective-permute-start.1 = (bf16[4,512,512]{2,1,0:T(8,128)(2,1)}, bf16[4,512,512]{2,1,0:T(8,128)(2,1)}, u32[]{:S(2)}, u32[]{:S(2)}) collective-permute-start(bf16[4,512,512]{2,1,0:T(8,128)(2,1)} %bitcast.16), channel_id=1, source_target_pairs={{0,1},{1,0},{2,3},{3,2},{4,5},{5,4},{6,7},{7,6},{8,9},{9,8},{10,11... | collective-permute-start | bytes 6291464 | tf_op jit(solution)/shard_map/ppermute | solution.py:173
  5.2 1.0 %and_select_fusion.1 = bf16[128,512]{1,0:T(8,128)(2,1)S(1)} fusion(bf16[1,512,512]{2,1,0:T(8,128)(2,1)} %param.6, s32[]{:T(128)S(6)} %select_n.38, pred[512]{0:T(512)(128)(4,1)S(1)} %iota_compare_fusion, pred[128]{0:T(512)(128)(4,1)S(1)} %add_compare_fusion), kind=kLoop, calls=%fused_computation.1 | loop fusion | flops 131072 | bytes 262788 | tf_op jit(solution)/shard_map/jit(_where)/select_n | solution.py:156
  6.2 15.1 %collective-permute-start.3 = (bf16[128,512]{1,0:T(8,128)(2,1)S(1)}, bf16[128,512]{1,0:T(8,128)(2,1)S(1)}, u32[]{:S(2)}, u32[]{:S(2)}) collective-permute-start(bf16[128,512]{1,0:T(8,128)(2,1)S(1)} %and_select_fusion.1), channel_id=1, source_target_pairs={{64,0},{66,2},{68,4},{70,6},{72,8},{74,10},{76,12},{78,14},{80,16}... | collective-permute-start | bytes 393224 | tf_op jit(solution)/shard_map/ppermute | solution.py:157
  21.3 0.7 collective-permute-start.4
  22.0 1.3 %and_select_fusion.rest_4_ = bf16[512,512]{1,0:T(8,128)(2,1)S(1)} fusion(bf16[1,512,512]{2,1,0:T(8,128)(2,1)} %param.6, pred[512]{0:T(512)(128)(4,1)S(1)} %iota_compare_fusion), kind=kLoop, calls=%fused_computation | loop fusion | flops 524288 | bytes 1049088 | tf_op jit(solution)/shard_map/jit(_where)/select_n | solution.py:160
  23.2 2.9 %collective-permute-start.6 = (bf16[512,512]{1,0:T(8,128)(2,1)S(1)}, bf16[512,512]{1,0:T(8,128)(2,1)S(1)}, u32[]{:S(2)}, u32[]{:S(2)}) collective-permute-start(bf16[512,512]{1,0:T(8,128)(2,1)S(1)} %and_select_fusion.rest_4_), channel_id=1, source_target_pairs={{8,0},{10,2},{12,4},{14,6},{16,8},{1,9},{18,10},{3,11},{20,12},{5,... | collective-permute-start | bytes 1572872 | tf_op jit(solution)/shard_map/ppermute | solution.py:161
  26.2 6.9 %collective-permute-done.3 = bf16[128,512]{1,0:T(8,128)(2,1)S(1)} collective-permute-done((bf16[128,512]{1,0:T(8,128)(2,1)S(1)}, bf16[128,512]{1,0:T(8,128)(2,1)S(1)}, u32[]{:S(2)}, u32[]{:S(2)}) %collective-permute-start.3) | collective-permute-done | bytes 131104 | tf_op jit(solution)/shard_map/ppermute | solution.py:157
  33.1 0.0 collective-permute-done.4
  33.1 0.8 %broadcast_in_dim.26 = bf16[4,128,512]{2,1,0:T(8,128)(2,1)} broadcast(bf16[128,512]{1,0:T(8,128)(2,1)S(1)} %broadcast_select_fusion), dimensions={1,2} | broadcast | bytes 655360 | tf_op jit(solution)/shard_map/broadcast_in_dim | solution.py:181
  33.9 4.5 %all-to-all-start = ((bf16[4,128,512]{2,1,0:T(8,128)(2,1)}), bf16[4,128,512]{2,1,0:T(8,128)(2,1)S(1)}, u32[]{:S(2)}, u32[]{:S(2)}) async-start(bf16[4,128,512]{2,1,0:T(8,128)(2,1)} %broadcast_in_dim.26), calls=%async_computation | async-start | bytes 1048576 | tf_op jit(solution)/shard_map/all_to_all | solution.py:182
  38.4 0.3 collective-permute-done.6.rest_5_
  38.7 2.4 %collective-permute-start.7 = (bf16[512,512]{1,0:T(8,128)(2,1)S(1)}, bf16[512,512]{1,0:T(8,128)(2,1)S(1)}, u32[]{:S(2)}, u32[]{:S(2)}) collective-permute-start(bf16[512,512]{1,0:T(8,128)(2,1)S(1)} %collective-permute-done.6.rest_5_), channel_id=1, source_target_pairs={{0,1},{1,0},{2,3},{3,2},{4,5},{5,4},{6,7},{7,6},{8,9},{9,8},{10,11... | collective-permute-start | bytes 1572872 | tf_op jit(solution)/shard_map/ppermute | solution.py:175
  41.1 8.0 %all-to-all-done = bf16[4,128,512]{2,1,0:T(8,128)(2,1)S(1)} async-done(((bf16[4,128,512]{2,1,0:T(8,128)(2,1)}), bf16[4,128,512]{2,1,0:T(8,128)(2,1)S(1)}, u32[]{:S(2)}, u32[]{:S(2)}) %all-to-all-start) | async-done | bytes 524320 | tf_op jit(solution)/shard_map/all_to_all | solution.py:182
  49.1 1.9 %collective-permute-start.5 = (bf16[512,512]{1,0:T(8,128)(2,1)S(1)}, bf16[512,512]{1,0:T(8,128)(2,1)S(1)}, u32[]{:S(2)}, u32[]{:S(2)}) collective-permute-start(bf16[512,512]{1,0:T(8,128)(2,1)S(1)} %bitcast.14), channel_id=1, source_target_pairs={{0,1},{1,0},{2,3},{3,2},{4,5},{5,4},{6,7},{7,6},{8,9},{9,8},{10,11... | collective-permute-start | bytes 1572872 | tf_op jit(solution)/shard_map/ppermute | solution.py:185
  51.1 0.1 compare_select_fusion.mine
  51.1 2.4 %collective-permute-start = (f32[8]{0:T(128)S(1)}, f32[8]{0:T(128)S(1)}, u32[]{:S(2)}, u32[]{:S(2)}) collective-permute-start(f32[8]{0:T(128)S(1)} %compare_select_fusion.mine), channel_id=1, source_target_pairs={{0,1},{1,0},{2,3},{3,2},{4,5},{5,4},{6,7},{7,6},{8,9},{9,8},{10,11... | collective-permute-start | bytes 104 | tf_op jit(solution)/shard_map/ppermute | solution.py:174
  53.5 0.8 %collective-permute-done.other = f32[8]{0:T(128)S(1)} collective-permute-done((f32[8]{0:T(128)S(1)}, f32[8]{0:T(128)S(1)}, u32[]{:S(2)}, u32[]{:S(2)}) %collective-permute-start) | collective-permute-done | bytes 64 | tf_op jit(solution)/shard_map/ppermute | solution.py:174
  54.3 0.0 collective-permute-done.7.rest_6_
  54.4 6.3 %shard_map.64.rest_6_ = f32[256,512]{1,0:T(8,128)S(1)} custom-call(s32[1]{0:T(128)} %copy.7.size, s32[1]{0:T(128)} %bitcast.parity, f32[8]{0:T(128)S(1)} %compare_select_fusion.mine, f32[8]{0:T(128)S(1)} %collective-permute-done.other, bf16[4,4,2,64,512]{4,3,2,1,0:T(8,128)(2,1)} %bitcast.17, bf16[4,4,2,64,512]{4,3,2,1,0:T(8,128)(2,1)} %bitcast.3.rest_1_, ...), custom_call_target="tpu_custom_call" | custom-call | flops 1610612736 | bytes 4194304 | tf_op jit(solution)/shard_map/pallas_call | solution.py:102
  60.7 0.0 collective-permute-done.5.rest_5_
  60.7 3.2 %shard_map.65 = f32[4,64,512]{2,1,0:T(8,128)S(1)} custom-call(s32[1]{0:T(128)} %copy.7.size, s32[1]{0:T(128)} %bitcast.parity, f32[8]{0:T(128)S(1)} %compare_select_fusion.mine, f32[8]{0:T(128)S(1)} %collective-permute-done.other, bf16[4,4,2,64,512]{4,3,2,1,0:T(8,128)(2,1)} %bitcast.18, bf16[4,4,2,64,512]{4,3,2,1,0:T(8,128)(2,1)} %bitcast.3.rest_1_, ...), custom_call_target="tpu_custom_call" | custom-call | flops 1610612736 | bytes 4194304 | tf_op jit(solution)/shard_map/pallas_call | solution.py:102
  63.9 12.7 %all_to_all.10 = f32[4,64,512]{2,1,0:T(8,128)S(1)} all-to-all(f32[4,64,512]{2,1,0:T(8,128)S(1)} %shard_map.65), channel_id=1, replica_groups={{0,2,4,6},{1,3,5,7},{8,10,12,14},{9,11,13,15},{16,18,20,22},{17,19,21,2..., dimensions={0} | all-to-all | bytes 1048576 | tf_op jit(solution)/shard_map/all_to_all | solution.py:187
  76.6 0.7 reduce_sum.9
  (9 shorter events, 0.0 us)
Async XLA Ops:
  0.0 51.1 %copy-start = (f32[4]{0:T(128)S(1)}, f32[4]{0:T(128)}, u32[]{:S(2)}) copy-start(f32[4]{0:T(128)} %param.10) | copy-start | bytes 52
  0.0 51.1 %copy-start.1 = (s32[4]{0:T(128)S(1)}, s32[4]{0:T(128)}, u32[]{:S(2)}) copy-start(s32[4]{0:T(128)} %param.9) | copy-start | bytes 52
  0.0 54.3 %collective-permute-start.2 = (bf16[4,512,512]{2,1,0:T(8,128)(2,1)}, bf16[4,512,512]{2,1,0:T(8,128)(2,1)}, u32[]{:S(2)}, u32[]{:S(2)}) collective-permute-start(bf16[4,512,512]{2,1,0:T(8,128)(2,1)} %bitcast.19), channel_id=1, source_target_pairs={{0,1},{1,0},{2,3},{3,2},{4,5},{5,4},{6,7},{7,6},{8,9},{9,8},{10,11... | collective-permute-start | bytes 6291464 | tf_op jit(solution)/shard_map/ppermute | solution.py:172
  2.1 52.3 %collective-permute-start.1 = (bf16[4,512,512]{2,1,0:T(8,128)(2,1)}, bf16[4,512,512]{2,1,0:T(8,128)(2,1)}, u32[]{:S(2)}, u32[]{:S(2)}) collective-permute-start(bf16[4,512,512]{2,1,0:T(8,128)(2,1)} %bitcast.16), channel_id=1, source_target_pairs={{0,1},{1,0},{2,3},{3,2},{4,5},{5,4},{6,7},{7,6},{8,9},{9,8},{10,11... | collective-permute-start | bytes 6291464 | tf_op jit(solution)/shard_map/ppermute | solution.py:173
  6.2 26.9 %collective-permute-start.3 = (bf16[128,512]{1,0:T(8,128)(2,1)S(1)}, bf16[128,512]{1,0:T(8,128)(2,1)S(1)}, u32[]{:S(2)}, u32[]{:S(2)}) collective-permute-start(bf16[128,512]{1,0:T(8,128)(2,1)S(1)} %and_select_fusion.1), channel_id=1, source_target_pairs={{64,0},{66,2},{68,4},{70,6},{72,8},{74,10},{76,12},{78,14},{80,16}... | collective-permute-start | bytes 393224 | tf_op jit(solution)/shard_map/ppermute | solution.py:157
  21.3 11.8 %collective-permute-start.4 = (bf16[128,512]{1,0:T(8,128)(2,1)S(1)}, bf16[128,512]{1,0:T(8,128)(2,1)S(1)}, u32[]{:S(2)}, u32[]{:S(2)}) collective-permute-start(bf16[128,512]{1,0:T(8,128)(2,1)S(1)} %and_select_fusion.1), channel_id=1, source_target_pairs={{1,65},{3,67},{5,69},{7,71},{9,73},{11,75},{13,77},{15,79},{17,81}... | collective-permute-start | bytes 393224 | tf_op jit(solution)/shard_map/ppermute | solution.py:158
  23.2 15.5 %collective-permute-start.6 = (bf16[512,512]{1,0:T(8,128)(2,1)S(1)}, bf16[512,512]{1,0:T(8,128)(2,1)S(1)}, u32[]{:S(2)}, u32[]{:S(2)}) collective-permute-start(bf16[512,512]{1,0:T(8,128)(2,1)S(1)} %and_select_fusion.rest_4_), channel_id=1, source_target_pairs={{8,0},{10,2},{12,4},{14,6},{16,8},{1,9},{18,10},{3,11},{20,12},{5,... | collective-permute-start | bytes 1572872 | tf_op jit(solution)/shard_map/ppermute | solution.py:161
  33.9 15.2 %all-to-all-start = ((bf16[4,128,512]{2,1,0:T(8,128)(2,1)}), bf16[4,128,512]{2,1,0:T(8,128)(2,1)S(1)}, u32[]{:S(2)}, u32[]{:S(2)}) async-start(bf16[4,128,512]{2,1,0:T(8,128)(2,1)} %broadcast_in_dim.26), calls=%async_computation | async-start | bytes 1048576 | tf_op jit(solution)/shard_map/all_to_all | solution.py:182
  38.7 15.7 %collective-permute-start.7 = (bf16[512,512]{1,0:T(8,128)(2,1)S(1)}, bf16[512,512]{1,0:T(8,128)(2,1)S(1)}, u32[]{:S(2)}, u32[]{:S(2)}) collective-permute-start(bf16[512,512]{1,0:T(8,128)(2,1)S(1)} %collective-permute-done.6.rest_5_), channel_id=1, source_target_pairs={{0,1},{1,0},{2,3},{3,2},{4,5},{5,4},{6,7},{7,6},{8,9},{9,8},{10,11... | collective-permute-start | bytes 1572872 | tf_op jit(solution)/shard_map/ppermute | solution.py:175
  49.1 11.5 %collective-permute-start.5 = (bf16[512,512]{1,0:T(8,128)(2,1)S(1)}, bf16[512,512]{1,0:T(8,128)(2,1)S(1)}, u32[]{:S(2)}, u32[]{:S(2)}) collective-permute-start(bf16[512,512]{1,0:T(8,128)(2,1)S(1)} %bitcast.14), channel_id=1, source_target_pairs={{0,1},{1,0},{2,3},{3,2},{4,5},{5,4},{6,7},{7,6},{8,9},{9,8},{10,11... | collective-permute-start | bytes 1572872 | tf_op jit(solution)/shard_map/ppermute | solution.py:185
  51.1 3.2 %collective-permute-start = (f32[8]{0:T(128)S(1)}, f32[8]{0:T(128)S(1)}, u32[]{:S(2)}, u32[]{:S(2)}) collective-permute-start(f32[8]{0:T(128)S(1)} %compare_select_fusion.mine), channel_id=1, source_target_pairs={{0,1},{1,0},{2,3},{3,2},{4,5},{5,4},{6,7},{7,6},{8,9},{9,8},{10,11... | collective-permute-start | bytes 104 | tf_op jit(solution)/shard_map/ppermute | solution.py:174

commit v3 on v2

--- a/solution.py
+++ b/solution.py
@@ -1,4 +1,5 @@
 import functools
+import math
 
 import jax
 import jax.numpy as jnp
@@ -10,6 +11,8 @@
 
 GRID = 8
 CORES = 2
+TOP = 14.0
+NOTE = 8
 EARLY = ((0.0, 0.0), (2.0, 1.0), (1.0, 2.0))
 LATE = ((4.0, 3.0), (3.0, 4.0))
 
@@ -83,11 +86,20 @@
     if early:
         out[...] = acc[...]
         return
+    largest = jnp.zeros((1, 1), jnp.float32)
     for y in range(chips):
         row = (y * CORES + core) * step + lax.broadcasted_iota(jnp.int32, (step, extent), 0)
         column = lax.broadcasted_iota(jnp.int32, (step, extent), 1)
         live = (row < size[0]) & (column < size[0])
-        out[y] = jnp.where(live, acc[pl.ds(y * step, step), :], 0.0)
+        rows = pl.ds(y * step, step)
+        value = jnp.where(live, acc[rows, :], 0.0)
+        acc[rows, :] = value
+        largest = jnp.maximum(largest, jnp.max(jnp.abs(value), axis=(0, 1), keepdims=True))
+    exponent = jnp.ceil(jnp.log(jnp.maximum(largest, 1e-30)) * (1 / math.log(2)))
+    factor = jnp.exp2(TOP - exponent)
+    for y in range(chips):
+        out[y, pl.ds(0, step), :] = acc[pl.ds(y * step, step), :] * factor
+        out[y, pl.ds(step, NOTE), :] = jnp.broadcast_to(exponent, (NOTE, extent))
 
 
 def terms(sources, before, size, parity, mine, other, lefts, rights):
@@ -96,7 +108,7 @@
     smem = pl.BlockSpec(memory_space=pltpu.SMEM)
     vmem = pl.BlockSpec(memory_space=pltpu.VMEM)
     anywhere = pl.BlockSpec(memory_space=pl.ANY)
-    shape = (chips * step, extent) if early else (chips, step, extent)
+    shape = (chips * step, extent) if early else (chips, step + NOTE, extent)
     held = sources if early else (*sources, before)
     held = [pltpu.with_memory_space_constraint(a, pltpu.VMEM) for a in held]
     return pl.pallas_call(
@@ -184,8 +196,11 @@
     early = terms((masked, near_one, near_two), None, *shared)
     far_two = lax.ppermute(far_one, "mpo", swap)
     half = terms((far_one, far_two), early, *shared)
+    half = half.astype(jnp.float16)
     pieces = lax.all_to_all(half, "mpo", 0, 0, axis_index_groups=same_core)
-    return jnp.sum(pieces, axis=0)[None]
+    pieces = pieces.astype(jnp.float32)
+    factor = jnp.exp2(pieces[:, step : step + 1] - TOP)
+    return jnp.sum(pieces[:, :step] * factor, axis=0)[None]
 
 
 def solution(mesh):

time: 77.7 us -> 75.6 us (0.973)
  blocking collectives: 12.7 us -> 10.2 us
    all_to_all x1, blocking collectives: 12.7 us -> 10.2 us  [per_device(): pieces = lax.all_to_all(half, 'mpo', 0, 0, axis_index_groups=same_core)]
where the time goes in v3:
time: 75.6 us; the launch traced here: 75.1 us
  starting transfers between devices  34.3 us (45%)
  waiting for transfers between devices  16 us (21%)
  blocking collectives  10.2 us (13%)
  Pallas kernels  9.67 us (13%)
  other arithmetic  3.21 us (4%)
  local copies, waits for them, and re-layouts  0.86 us (1%)
  between operations  0.85 us (1%)
    ppermute x1, starting transfers between devices, per_device(): above_strip = lax.ppermute(strip, both, far_above)  15.1 us
    all_to_all x1, blocking collectives, per_device(): pieces = lax.all_to_all(half, 'mpo', 0, 0, axis_index_groups=same_core)  10.2 us
    pallas_call x2, Pallas kernels, terms(): pl.pallas_call(functools.partial(terms_kernel, early), out_shape=jax.Shap...  9.67 us
    all_to_all x1, waiting for transfers between devices, per_device(): far_one = lax.all_to_all(spread, 'mpo', 0, 0, axis_index_groups=same_core)  8.01 us
    ppermute x1, waiting for transfers between devices, per_device(): above_strip = lax.ppermute(strip, both, far_above)  6.91 us
    all_to_all x1, starting transfers between devices, per_device(): far_one = lax.all_to_all(spread, 'mpo', 0, 0, axis_index_groups=same_core)  4.46 us
    ppermute x1, starting transfers between devices, per_device(): near_one = lax.ppermute(masked, both, near)  2.92 us
    ppermute x1, starting transfers between devices, per_device(): near_two = lax.ppermute(near_one, 'mpo', swap)  2.42 us
  transfers between devices with their start and end apart: 9, of which 4 were waited for; matrix products, arithmetic and copies ran while one was open for 4% of the time, Pallas kernels for 8%

profile of v3, /device:TPU:38, one launch (start us, length us, event | category | flops | bytes accessed | tf_op | source)
XLA Modules:
  0.0 75.1 jit_solution(16936737054856210931)
XLA Ops:
  0.0 2.0 %collective-permute-start.2 = (bf16[4,512,512]{2,1,0:T(8,128)(2,1)}, bf16[4,512,512]{2,1,0:T(8,128)(2,1)}, u32[]{:S(2)}, u32[]{:S(2)}) collective-permute-start(bf16[4,512,512]{2,1,0:T(8,128)(2,1)} %bitcast.22), channel_id=1, source_target_pairs={{0,1},{1,0},{2,3},{3,2},{4,5},{5,4},{6,7},{7,6},{8,9},{9,8},{10,11... | collective-permute-start | bytes 6291464 | tf_op jit(solution)/shard_map/ppermute | solution.py:184
  2.1 2.4 %collective-permute-start.1 = (bf16[4,512,512]{2,1,0:T(8,128)(2,1)}, bf16[4,512,512]{2,1,0:T(8,128)(2,1)}, u32[]{:S(2)}, u32[]{:S(2)}) collective-permute-start(bf16[4,512,512]{2,1,0:T(8,128)(2,1)} %bitcast.19), channel_id=1, source_target_pairs={{0,1},{1,0},{2,3},{3,2},{4,5},{5,4},{6,7},{7,6},{8,9},{9,8},{10,11... | collective-permute-start | bytes 6291464 | tf_op jit(solution)/shard_map/ppermute | solution.py:185
  5.2 1.0 %and_select_fusion.1 = bf16[128,512]{1,0:T(8,128)(2,1)S(1)} fusion(bf16[1,512,512]{2,1,0:T(8,128)(2,1)} %param.6, s32[]{:T(128)S(6)} %select_n.38, pred[512]{0:T(512)(128)(4,1)S(1)} %iota_compare_fusion, pred[128]{0:T(512)(128)(4,1)S(1)} %add_compare_fusion), kind=kLoop, calls=%fused_computation.3 | loop fusion | flops 131072 | bytes 262788 | tf_op jit(solution)/shard_map/jit(_where)/select_n | solution.py:168
  6.2 15.1 %collective-permute-start.3 = (bf16[128,512]{1,0:T(8,128)(2,1)S(1)}, bf16[128,512]{1,0:T(8,128)(2,1)S(1)}, u32[]{:S(2)}, u32[]{:S(2)}) collective-permute-start(bf16[128,512]{1,0:T(8,128)(2,1)S(1)} %and_select_fusion.1), channel_id=1, source_target_pairs={{64,0},{66,2},{68,4},{70,6},{72,8},{74,10},{76,12},{78,14},{80,16}... | collective-permute-start | bytes 393224 | tf_op jit(solution)/shard_map/ppermute | solution.py:169
  21.3 0.7 collective-permute-start.4
  22.0 1.3 %and_select_fusion.rest_4_ = bf16[512,512]{1,0:T(8,128)(2,1)S(1)} fusion(bf16[1,512,512]{2,1,0:T(8,128)(2,1)} %param.6, pred[512]{0:T(512)(128)(4,1)S(1)} %iota_compare_fusion), kind=kLoop, calls=%fused_computation | loop fusion | flops 524288 | bytes 1049088 | tf_op jit(solution)/shard_map/jit(_where)/select_n | solution.py:172
  23.2 2.9 %collective-permute-start.6 = (bf16[512,512]{1,0:T(8,128)(2,1)S(1)}, bf16[512,512]{1,0:T(8,128)(2,1)S(1)}, u32[]{:S(2)}, u32[]{:S(2)}) collective-permute-start(bf16[512,512]{1,0:T(8,128)(2,1)S(1)} %and_select_fusion.rest_4_), channel_id=1, source_target_pairs={{8,0},{10,2},{12,4},{14,6},{16,8},{1,9},{18,10},{3,11},{20,12},{5,... | collective-permute-start | bytes 1572872 | tf_op jit(solution)/shard_map/ppermute | solution.py:173
  26.2 6.9 %collective-permute-done.3 = bf16[128,512]{1,0:T(8,128)(2,1)S(1)} collective-permute-done((bf16[128,512]{1,0:T(8,128)(2,1)S(1)}, bf16[128,512]{1,0:T(8,128)(2,1)S(1)}, u32[]{:S(2)}, u32[]{:S(2)}) %collective-permute-start.3) | collective-permute-done | bytes 131104 | tf_op jit(solution)/shard_map/ppermute | solution.py:169
  33.1 0.0 collective-permute-done.4
  33.1 0.8 %broadcast_in_dim.26 = bf16[4,128,512]{2,1,0:T(8,128)(2,1)} broadcast(bf16[128,512]{1,0:T(8,128)(2,1)S(1)} %broadcast_select_fusion), dimensions={1,2} | broadcast | bytes 655360 | tf_op jit(solution)/shard_map/broadcast_in_dim | solution.py:193
  33.9 4.5 %all-to-all-start = ((bf16[4,128,512]{2,1,0:T(8,128)(2,1)}), bf16[4,128,512]{2,1,0:T(8,128)(2,1)S(1)}, u32[]{:S(2)}, u32[]{:S(2)}) async-start(bf16[4,128,512]{2,1,0:T(8,128)(2,1)} %broadcast_in_dim.26), calls=%async_computation | async-start | bytes 1048576 | tf_op jit(solution)/shard_map/all_to_all | solution.py:194
  38.4 0.3 collective-permute-done.6.rest_5_
  38.7 2.4 %collective-permute-start.7 = (bf16[512,512]{1,0:T(8,128)(2,1)S(1)}, bf16[512,512]{1,0:T(8,128)(2,1)S(1)}, u32[]{:S(2)}, u32[]{:S(2)}) collective-permute-start(bf16[512,512]{1,0:T(8,128)(2,1)S(1)} %collective-permute-done.6.rest_5_), channel_id=1, source_target_pairs={{0,1},{1,0},{2,3},{3,2},{4,5},{5,4},{6,7},{7,6},{8,9},{9,8},{10,11... | collective-permute-start | bytes 1572872 | tf_op jit(solution)/shard_map/ppermute | solution.py:187
  41.1 8.0 %all-to-all-done = bf16[4,128,512]{2,1,0:T(8,128)(2,1)S(1)} async-done(((bf16[4,128,512]{2,1,0:T(8,128)(2,1)}), bf16[4,128,512]{2,1,0:T(8,128)(2,1)S(1)}, u32[]{:S(2)}, u32[]{:S(2)}) %all-to-all-start) | async-done | bytes 524320 | tf_op jit(solution)/shard_map/all_to_all | solution.py:194
  49.1 1.9 %collective-permute-start.5 = (bf16[512,512]{1,0:T(8,128)(2,1)S(1)}, bf16[512,512]{1,0:T(8,128)(2,1)S(1)}, u32[]{:S(2)}, u32[]{:S(2)}) collective-permute-start(bf16[512,512]{1,0:T(8,128)(2,1)S(1)} %bitcast.17), channel_id=1, source_target_pairs={{0,1},{1,0},{2,3},{3,2},{4,5},{5,4},{6,7},{7,6},{8,9},{9,8},{10,11... | collective-permute-start | bytes 1572872 | tf_op jit(solution)/shard_map/ppermute | solution.py:197
  51.1 0.1 compare_select_fusion.mine
  51.1 2.4 %collective-permute-start = (f32[8]{0:T(128)S(1)}, f32[8]{0:T(128)S(1)}, u32[]{:S(2)}, u32[]{:S(2)}) collective-permute-start(f32[8]{0:T(128)S(1)} %compare_select_fusion.mine), channel_id=1, source_target_pairs={{0,1},{1,0},{2,3},{3,2},{4,5},{5,4},{6,7},{7,6},{8,9},{9,8},{10,11... | collective-permute-start | bytes 104 | tf_op jit(solution)/shard_map/ppermute | solution.py:186
  53.5 0.8 %collective-permute-done.other = f32[8]{0:T(128)S(1)} collective-permute-done((f32[8]{0:T(128)S(1)}, f32[8]{0:T(128)S(1)}, u32[]{:S(2)}, u32[]{:S(2)}) %collective-permute-start) | collective-permute-done | bytes 64 | tf_op jit(solution)/shard_map/ppermute | solution.py:186
  54.4 6.3 %shard_map.64.rest_6_ = f32[256,512]{1,0:T(8,128)S(1)} custom-call(s32[1]{0:T(128)} %copy.10.size, s32[1]{0:T(128)} %bitcast.parity, f32[8]{0:T(128)S(1)} %compare_select_fusion.mine, f32[8]{0:T(128)S(1)} %collective-permute-done.other, bf16[4,4,2,64,512]{4,3,2,1,0:T(8,128)(2,1)} %bitcast.20, bf16[4,4,2,64,512]{4,3,2,1,0:T(8,128)(2,1)} %bitcast.3.rest_1_, ...), custom_call_target="tpu_custom_call" | custom-call | flops 1610612736 | bytes 4194304 | tf_op jit(solution)/shard_map/pallas_call | solution.py:114
  60.7 0.0 collective-permute-done.5.rest_5_
  60.7 3.4 %shard_map.65 = f32[4,72,512]{2,1,0:T(8,128)S(1)} custom-call(s32[1]{0:T(128)} %copy.10.size, s32[1]{0:T(128)} %bitcast.parity, f32[8]{0:T(128)S(1)} %compare_select_fusion.mine, f32[8]{0:T(128)S(1)} %collective-permute-done.other, bf16[4,4,2,64,512]{4,3,2,1,0:T(8,128)(2,1)} %bitcast.21, bf16[4,4,2,64,512]{4,3,2,1,0:T(8,128)(2,1)} %bitcast.3.rest_1_, ...), custom_call_target="tpu_custom_call" | custom-call | flops 1610612736 | bytes 4194304 | tf_op jit(solution)/shard_map/pallas_call | solution.py:114
  64.1 10.2 %all_to_all.10 = f16[4,72,512]{2,1,0:T(8,128)(2,1)S(1)} all-to-all(f16[4,72,512]{2,1,0:T(8,128)(2,1)S(1)} %convert_element_type.16), channel_id=1, replica_groups={{0,2,4,6},{1,3,5,7},{8,10,12,14},{9,11,13,15},{16,18,20,22},{17,19,21,2..., dimensions={0} | all-to-all | bytes 589824 | tf_op jit(solution)/shard_map/all_to_all | solution.py:200
  74.3 0.1 convert_element_type.17
  74.4 0.7 fusion
  (13 shorter events, 0.1 us)
Async XLA Ops:
  0.0 51.1 %copy-start = (f32[4]{0:T(128)S(1)}, f32[4]{0:T(128)}, u32[]{:S(2)}) copy-start(f32[4]{0:T(128)} %param.10) | copy-start | bytes 52
  0.0 51.1 %copy-start.1 = (s32[4]{0:T(128)S(1)}, s32[4]{0:T(128)}, u32[]{:S(2)}) copy-start(s32[4]{0:T(128)} %param.9) | copy-start | bytes 52
  0.0 54.3 %collective-permute-start.2 = (bf16[4,512,512]{2,1,0:T(8,128)(2,1)}, bf16[4,512,512]{2,1,0:T(8,128)(2,1)}, u32[]{:S(2)}, u32[]{:S(2)}) collective-permute-start(bf16[4,512,512]{2,1,0:T(8,128)(2,1)} %bitcast.22), channel_id=1, source_target_pairs={{0,1},{1,0},{2,3},{3,2},{4,5},{5,4},{6,7},{7,6},{8,9},{9,8},{10,11... | collective-permute-start | bytes 6291464 | tf_op jit(solution)/shard_map/ppermute | solution.py:184
  2.1 52.3 %collective-permute-start.1 = (bf16[4,512,512]{2,1,0:T(8,128)(2,1)}, bf16[4,512,512]{2,1,0:T(8,128)(2,1)}, u32[]{:S(2)}, u32[]{:S(2)}) collective-permute-start(bf16[4,512,512]{2,1,0:T(8,128)(2,1)} %bitcast.19), channel_id=1, source_target_pairs={{0,1},{1,0},{2,3},{3,2},{4,5},{5,4},{6,7},{7,6},{8,9},{9,8},{10,11... | collective-permute-start | bytes 6291464 | tf_op jit(solution)/shard_map/ppermute | solution.py:185
  6.2 26.9 %collective-permute-start.3 = (bf16[128,512]{1,0:T(8,128)(2,1)S(1)}, bf16[128,512]{1,0:T(8,128)(2,1)S(1)}, u32[]{:S(2)}, u32[]{:S(2)}) collective-permute-start(bf16[128,512]{1,0:T(8,128)(2,1)S(1)} %and_select_fusion.1), channel_id=1, source_target_pairs={{64,0},{66,2},{68,4},{70,6},{72,8},{74,10},{76,12},{78,14},{80,16}... | collective-permute-start | bytes 393224 | tf_op jit(solution)/shard_map/ppermute | solution.py:169
  21.3 11.8 %collective-permute-start.4 = (bf16[128,512]{1,0:T(8,128)(2,1)S(1)}, bf16[128,512]{1,0:T(8,128)(2,1)S(1)}, u32[]{:S(2)}, u32[]{:S(2)}) collective-permute-start(bf16[128,512]{1,0:T(8,128)(2,1)S(1)} %and_select_fusion.1), channel_id=1, source_target_pairs={{1,65},{3,67},{5,69},{7,71},{9,73},{11,75},{13,77},{15,79},{17,81}... | collective-permute-start | bytes 393224 | tf_op jit(solution)/shard_map/ppermute | solution.py:170
  23.2 15.5 %collective-permute-start.6 = (bf16[512,512]{1,0:T(8,128)(2,1)S(1)}, bf16[512,512]{1,0:T(8,128)(2,1)S(1)}, u32[]{:S(2)}, u32[]{:S(2)}) collective-permute-start(bf16[512,512]{1,0:T(8,128)(2,1)S(1)} %and_select_fusion.rest_4_), channel_id=1, source_target_pairs={{8,0},{10,2},{12,4},{14,6},{16,8},{1,9},{18,10},{3,11},{20,12},{5,... | collective-permute-start | bytes 1572872 | tf_op jit(solution)/shard_map/ppermute | solution.py:173
  33.9 15.2 %all-to-all-start = ((bf16[4,128,512]{2,1,0:T(8,128)(2,1)}), bf16[4,128,512]{2,1,0:T(8,128)(2,1)S(1)}, u32[]{:S(2)}, u32[]{:S(2)}) async-start(bf16[4,128,512]{2,1,0:T(8,128)(2,1)} %broadcast_in_dim.26), calls=%async_computation | async-start | bytes 1048576 | tf_op jit(solution)/shard_map/all_to_all | solution.py:194
  38.7 15.7 %collective-permute-start.7 = (bf16[512,512]{1,0:T(8,128)(2,1)S(1)}, bf16[512,512]{1,0:T(8,128)(2,1)S(1)}, u32[]{:S(2)}, u32[]{:S(2)}) collective-permute-start(bf16[512,512]{1,0:T(8,128)(2,1)S(1)} %collective-permute-done.6.rest_5_), channel_id=1, source_target_pairs={{0,1},{1,0},{2,3},{3,2},{4,5},{5,4},{6,7},{7,6},{8,9},{9,8},{10,11... | collective-permute-start | bytes 1572872 | tf_op jit(solution)/shard_map/ppermute | solution.py:187
  49.1 11.5 %collective-permute-start.5 = (bf16[512,512]{1,0:T(8,128)(2,1)S(1)}, bf16[512,512]{1,0:T(8,128)(2,1)S(1)}, u32[]{:S(2)}, u32[]{:S(2)}) collective-permute-start(bf16[512,512]{1,0:T(8,128)(2,1)S(1)} %bitcast.17), channel_id=1, source_target_pairs={{0,1},{1,0},{2,3},{3,2},{4,5},{5,4},{6,7},{7,6},{8,9},{9,8},{10,11... | collective-permute-start | bytes 1572872 | tf_op jit(solution)/shard_map/ppermute | solution.py:197
  51.1 3.2 %collective-permute-start = (f32[8]{0:T(128)S(1)}, f32[8]{0:T(128)S(1)}, u32[]{:S(2)}, u32[]{:S(2)}) collective-permute-start(f32[8]{0:T(128)S(1)} %compare_select_fusion.mine), channel_id=1, source_target_pairs={{0,1},{1,0},{2,3},{3,2},{4,5},{5,4},{6,7},{7,6},{8,9},{9,8},{10,11... | collective-permute-start | bytes 104 | tf_op jit(solution)/shard_map/ppermute | solution.py:186

commit v4 on v3

--- a/solution.py
+++ b/solution.py
@@ -17,16 +17,17 @@
 LATE = ((4.0, 3.0), (3.0, 4.0))
 
 
-def terms_kernel(early, size, parity, mine, other, *rest):
+def terms_kernel(early, mine, other, *rest):
     lefts, rights, rest = rest[0:2], rest[2:4], rest[4:]
     codes = EARLY if early else LATE
     n = len(codes)
     sources, rest = rest[:n], rest[n:]
     if not early:
         before, rest = rest[0], rest[1:]
-    out, left_buf, right_buf, acc, scale, sems = rest
+    out, left_buf, right_buf, scale, sems, *rest = rest
+    acc = out if early else rest[0]
     count, (chips, step, extent) = left_buf.shape[0] // 2, left_buf.shape[1:]
-    core = parity[0]
+    core, size = mine[2 * count].astype(jnp.int32), mine[2 * count + 1].astype(jnp.int32)
 
     def fetch_left(k, w, at):
         return pltpu.make_async_copy(lefts[k].at[w, :, core], left_buf.at[at], sems.at[0, at])
@@ -84,13 +85,12 @@
             add(source, (end - 1,))
 
     if early:
-        out[...] = acc[...]
         return
     largest = jnp.zeros((1, 1), jnp.float32)
     for y in range(chips):
         row = (y * CORES + core) * step + lax.broadcasted_iota(jnp.int32, (step, extent), 0)
         column = lax.broadcasted_iota(jnp.int32, (step, extent), 1)
-        live = (row < size[0]) & (column < size[0])
+        live = (row < size) & (column < size)
         rows = pl.ds(y * step, step)
         value = jnp.where(live, acc[rows, :], 0.0)
         acc[rows, :] = value
@@ -102,7 +102,7 @@
         out[y, pl.ds(step, NOTE), :] = jnp.broadcast_to(exponent, (NOTE, extent))
 
 
-def terms(sources, before, size, parity, mine, other, lefts, rights):
+def terms(sources, before, mine, other, lefts, rights):
     early = before is None
     count, chips, _, step, extent = lefts[0].shape
     smem = pl.BlockSpec(memory_space=pltpu.SMEM)
@@ -114,20 +114,20 @@
     return pl.pallas_call(
         functools.partial(terms_kernel, early),
         out_shape=jax.ShapeDtypeStruct(shape, jnp.float32),
-        in_specs=[smem] * 4 + [anywhere] * 4 + [vmem] * len(held),
+        in_specs=[smem] * 2 + [anywhere] * 4 + [vmem] * len(held),
         out_specs=vmem,
         scratch_shapes=[
             pltpu.VMEM((2 * count, chips, step, extent), jnp.bfloat16),
             pltpu.VMEM((2 * count, extent, extent), jnp.bfloat16),
-            pltpu.VMEM((chips * step, extent), jnp.float32),
             pltpu.SMEM((2 * count,), jnp.float32),
             pltpu.SemaphoreType.DMA((2, 2 * count)),
-        ],
+        ]
+        + ([] if early else [pltpu.VMEM((chips * step, extent), jnp.float32)]),
         compiler_params=pltpu.CompilerParams(vmem_limit_bytes=16 << 20),
         cost_estimate=pl.CostEstimate(
             flops=count * extent**3 * 3, bytes_accessed=count * extent**2 * 4, transcendentals=0
         ),
-    )(size, parity, mine, other, *lefts, *rights, *held)
+    )(mine, other, *lefts, *rights, *held)
 
 
 def per_device(
@@ -176,18 +176,20 @@
     by_core = lambda a: in_hbm(a.reshape(a.shape[0], chips, CORES, step, extent))
     left, right = left_environment[:, 0], right_environment[:, 0]
     count = coupling.shape[0]
+    lane = jnp.arange(2 * count + 2)
     mine = jnp.where(
-        jnp.arange(2 * count) < count,
-        jnp.pad(term_shift, (0, count)).astype(jnp.float32),
-        jnp.pad(coupling, (count, 0)),
-    )
+        lane < count,
+        jnp.pad(term_shift, (0, count + 2)).astype(jnp.float32),
+        jnp.where(lane < 2 * count, jnp.pad(coupling, (count, 2)), size.astype(jnp.float32)),
+    )
+    mine = jnp.where(lane == 2 * count, parity.astype(jnp.float32), mine)
     right_other = lax.ppermute(right, "mpo", swap)
     left_other = lax.ppermute(left, "mpo", swap)
     other = lax.ppermute(mine, "mpo", swap)
     near_two = lax.ppermute(near_one, "mpo", swap)
     lefts = (by_core(left), by_core(left_other))
     rights = (in_hbm(right), in_hbm(right_other))
-    shared = (block_sizes, parity[None].astype(jnp.int32), mine, other, lefts, rights)
+    shared = (mine, other, lefts, rights)
 
     far_strip = jnp.where(parity == 0, above_strip, below_strip)
     spread = jnp.broadcast_to(far_strip[None], (chips,) + far_strip.shape)

time: 75.6 us -> 75.6 us (level)
  no operation moved by 1% of the time
where the time goes in v4:
time: 75.6 us; the launch traced here: 75.1 us
  starting transfers between devices  34.3 us (45%)
  waiting for transfers between devices  16 us (21%)
  blocking collectives  10.2 us (13%)
  Pallas kernels  9.65 us (13%)
  other arithmetic  3.21 us (4%)
  local copies, waits for them, and re-layouts  0.86 us (1%)
  between operations  0.86 us (1%)
    ppermute x1, starting transfers between devices, per_device(): above_strip = lax.ppermute(strip, both, far_above)  15.1 us
    all_to_all x1, blocking collectives, per_device(): pieces = lax.all_to_all(half, 'mpo', 0, 0, axis_index_groups=same_core)  10.2 us
    pallas_call x2, Pallas kernels, terms(): pl.pallas_call(functools.partial(terms_kernel, early), out_shape=jax.Shap...  9.65 us
    all_to_all x1, waiting for transfers between devices, per_device(): far_one = lax.all_to_all(spread, 'mpo', 0, 0, axis_index_groups=same_core)  8.01 us
    ppermute x1, waiting for transfers between devices, per_device(): above_strip = lax.ppermute(strip, both, far_above)  6.91 us
    all_to_all x1, starting transfers between devices, per_device(): far_one = lax.all_to_all(spread, 'mpo', 0, 0, axis_index_groups=same_core)  4.46 us
    ppermute x1, starting transfers between devices, per_device(): near_one = lax.ppermute(masked, both, near)  2.92 us
    ppermute x1, starting transfers between devices, per_device(): near_two = lax.ppermute(near_one, 'mpo', swap)  2.42 us
  transfers between devices with their start and end apart: 9, of which 4 were waited for; matrix products, arithmetic and copies ran while one was open for 4% of the time, Pallas kernels for 8%

profile of v4, /device:TPU:38, one launch (start us, length us, event | category | flops | bytes accessed | tf_op | source)
XLA Modules:
  0.0 75.1 jit_solution(16107833968766675223)
XLA Ops:
  0.0 2.0 %collective-permute-start.2 = (bf16[4,512,512]{2,1,0:T(8,128)(2,1)}, bf16[4,512,512]{2,1,0:T(8,128)(2,1)}, u32[]{:S(2)}, u32[]{:S(2)}) collective-permute-start(bf16[4,512,512]{2,1,0:T(8,128)(2,1)} %bitcast.22), channel_id=1, source_target_pairs={{0,1},{1,0},{2,3},{3,2},{4,5},{5,4},{6,7},{7,6},{8,9},{9,8},{10,11... | collective-permute-start | bytes 6291464 | tf_op jit(solution)/shard_map/ppermute | solution.py:186
  2.1 2.4 %collective-permute-start.1 = (bf16[4,512,512]{2,1,0:T(8,128)(2,1)}, bf16[4,512,512]{2,1,0:T(8,128)(2,1)}, u32[]{:S(2)}, u32[]{:S(2)}) collective-permute-start(bf16[4,512,512]{2,1,0:T(8,128)(2,1)} %bitcast.19), channel_id=1, source_target_pairs={{0,1},{1,0},{2,3},{3,2},{4,5},{5,4},{6,7},{7,6},{8,9},{9,8},{10,11... | collective-permute-start | bytes 6291464 | tf_op jit(solution)/shard_map/ppermute | solution.py:187
  5.2 1.0 %and_select_fusion.1 = bf16[128,512]{1,0:T(8,128)(2,1)S(1)} fusion(bf16[1,512,512]{2,1,0:T(8,128)(2,1)} %param.6, s32[]{:T(128)S(6)} %select_n.48, pred[512]{0:T(512)(128)(4,1)S(1)} %iota_compare_fusion, pred[128]{0:T(512)(128)(4,1)S(1)} %add_compare_fusion), kind=kLoop, calls=%fused_computation.3 | loop fusion | flops 131072 | bytes 262788 | tf_op jit(solution)/shard_map/jit(_where)/select_n | solution.py:168
  6.2 15.1 %collective-permute-start.3 = (bf16[128,512]{1,0:T(8,128)(2,1)S(1)}, bf16[128,512]{1,0:T(8,128)(2,1)S(1)}, u32[]{:S(2)}, u32[]{:S(2)}) collective-permute-start(bf16[128,512]{1,0:T(8,128)(2,1)S(1)} %and_select_fusion.1), channel_id=1, source_target_pairs={{64,0},{66,2},{68,4},{70,6},{72,8},{74,10},{76,12},{78,14},{80,16}... | collective-permute-start | bytes 393224 | tf_op jit(solution)/shard_map/ppermute | solution.py:169
  21.3 0.7 collective-permute-start.4
  22.0 1.3 %and_select_fusion.rest_4_ = bf16[512,512]{1,0:T(8,128)(2,1)S(1)} fusion(bf16[1,512,512]{2,1,0:T(8,128)(2,1)} %param.6, pred[512]{0:T(512)(128)(4,1)S(1)} %iota_compare_fusion), kind=kLoop, calls=%fused_computation | loop fusion | flops 524288 | bytes 1049088 | tf_op jit(solution)/shard_map/jit(_where)/select_n | solution.py:172
  23.2 2.9 %collective-permute-start.6 = (bf16[512,512]{1,0:T(8,128)(2,1)S(1)}, bf16[512,512]{1,0:T(8,128)(2,1)S(1)}, u32[]{:S(2)}, u32[]{:S(2)}) collective-permute-start(bf16[512,512]{1,0:T(8,128)(2,1)S(1)} %and_select_fusion.rest_4_), channel_id=1, source_target_pairs={{8,0},{10,2},{12,4},{14,6},{16,8},{1,9},{18,10},{3,11},{20,12},{5,... | collective-permute-start | bytes 1572872 | tf_op jit(solution)/shard_map/ppermute | solution.py:173
  26.2 6.9 %collective-permute-done.3 = bf16[128,512]{1,0:T(8,128)(2,1)S(1)} collective-permute-done((bf16[128,512]{1,0:T(8,128)(2,1)S(1)}, bf16[128,512]{1,0:T(8,128)(2,1)S(1)}, u32[]{:S(2)}, u32[]{:S(2)}) %collective-permute-start.3) | collective-permute-done | bytes 131104 | tf_op jit(solution)/shard_map/ppermute | solution.py:169
  33.1 0.0 collective-permute-done.4
  33.1 0.8 %broadcast_in_dim.32 = bf16[4,128,512]{2,1,0:T(8,128)(2,1)} broadcast(bf16[128,512]{1,0:T(8,128)(2,1)S(1)} %broadcast_select_fusion), dimensions={1,2} | broadcast | bytes 655360 | tf_op jit(solution)/shard_map/broadcast_in_dim | solution.py:195
  33.9 4.5 %all-to-all-start = ((bf16[4,128,512]{2,1,0:T(8,128)(2,1)}), bf16[4,128,512]{2,1,0:T(8,128)(2,1)S(1)}, u32[]{:S(2)}, u32[]{:S(2)}) async-start(bf16[4,128,512]{2,1,0:T(8,128)(2,1)} %broadcast_in_dim.32), calls=%async_computation | async-start | bytes 1048576 | tf_op jit(solution)/shard_map/all_to_all | solution.py:196
  38.4 0.3 collective-permute-done.6.rest_5_
  38.7 2.4 %collective-permute-start.7 = (bf16[512,512]{1,0:T(8,128)(2,1)S(1)}, bf16[512,512]{1,0:T(8,128)(2,1)S(1)}, u32[]{:S(2)}, u32[]{:S(2)}) collective-permute-start(bf16[512,512]{1,0:T(8,128)(2,1)S(1)} %collective-permute-done.6.rest_5_), channel_id=1, source_target_pairs={{0,1},{1,0},{2,3},{3,2},{4,5},{5,4},{6,7},{7,6},{8,9},{9,8},{10,11... | collective-permute-start | bytes 1572872 | tf_op jit(solution)/shard_map/ppermute | solution.py:189
  41.1 8.0 %all-to-all-done = bf16[4,128,512]{2,1,0:T(8,128)(2,1)S(1)} async-done(((bf16[4,128,512]{2,1,0:T(8,128)(2,1)}), bf16[4,128,512]{2,1,0:T(8,128)(2,1)S(1)}, u32[]{:S(2)}, u32[]{:S(2)}) %all-to-all-start) | async-done | bytes 524320 | tf_op jit(solution)/shard_map/all_to_all | solution.py:196
  49.1 1.9 %collective-permute-start.5 = (bf16[512,512]{1,0:T(8,128)(2,1)S(1)}, bf16[512,512]{1,0:T(8,128)(2,1)S(1)}, u32[]{:S(2)}, u32[]{:S(2)}) collective-permute-start(bf16[512,512]{1,0:T(8,128)(2,1)S(1)} %bitcast.17), channel_id=1, source_target_pairs={{0,1},{1,0},{2,3},{3,2},{4,5},{5,4},{6,7},{7,6},{8,9},{9,8},{10,11... | collective-permute-start | bytes 1572872 | tf_op jit(solution)/shard_map/ppermute | solution.py:199
  51.1 0.1 compare_select_fusion.2.mine
  51.2 2.4 %collective-permute-start = (f32[10]{0:T(128)S(1)}, f32[10]{0:T(128)S(1)}, u32[]{:S(2)}, u32[]{:S(2)}) collective-permute-start(f32[10]{0:T(128)S(1)} %compare_select_fusion.2.mine), channel_id=1, source_target_pairs={{0,1},{1,0},{2,3},{3,2},{4,5},{5,4},{6,7},{7,6},{8,9},{9,8},{10,11... | collective-permute-start | bytes 128 | tf_op jit(solution)/shard_map/ppermute | solution.py:188
  53.6 0.8 %collective-permute-done.other = f32[10]{0:T(128)S(1)} collective-permute-done((f32[10]{0:T(128)S(1)}, f32[10]{0:T(128)S(1)}, u32[]{:S(2)}, u32[]{:S(2)}) %collective-permute-start) | collective-permute-done | bytes 72 | tf_op jit(solution)/shard_map/ppermute | solution.py:188
  54.4 6.3 %shard_map.64.rest_6_ = f32[256,512]{1,0:T(8,128)S(1)} custom-call(f32[10]{0:T(128)S(1)} %compare_select_fusion.2.mine, f32[10]{0:T(128)S(1)} %collective-permute-done.other, bf16[4,4,2,64,512]{4,3,2,1,0:T(8,128)(2,1)} %bitcast.20, bf16[4,4,2,64,512]{4,3,2,1,0:T(8,128)(2,1)} %bitcast.3.rest_1_, bf16[4,512,512]{2,1,0:T(8,128)(2,1)} %bitcast.23, ...), custom_call_target="tpu_custom_call" | custom-call | flops 1610612736 | bytes 4194304 | tf_op jit(solution)/shard_map/pallas_call | solution.py:114
  60.7 0.0 collective-permute-done.5.rest_5_
  60.7 3.4 %shard_map.65 = f32[4,72,512]{2,1,0:T(8,128)S(1)} custom-call(f32[10]{0:T(128)S(1)} %compare_select_fusion.2.mine, f32[10]{0:T(128)S(1)} %collective-permute-done.other, bf16[4,4,2,64,512]{4,3,2,1,0:T(8,128)(2,1)} %bitcast.21, bf16[4,4,2,64,512]{4,3,2,1,0:T(8,128)(2,1)} %bitcast.3.rest_1_, bf16[4,512,512]{2,1,0:T(8,128)(2,1)} %bitcast.24, ...), custom_call_target="tpu_custom_call" | custom-call | flops 1610612736 | bytes 4194304 | tf_op jit(solution)/shard_map/pallas_call | solution.py:114
  64.1 10.2 %all_to_all.10 = f16[4,72,512]{2,1,0:T(8,128)(2,1)S(1)} all-to-all(f16[4,72,512]{2,1,0:T(8,128)(2,1)S(1)} %convert_element_type.24), channel_id=1, replica_groups={{0,2,4,6},{1,3,5,7},{8,10,12,14},{9,11,13,15},{16,18,20,22},{17,19,21,2..., dimensions={0} | all-to-all | bytes 589824 | tf_op jit(solution)/shard_map/all_to_all | solution.py:202
  74.3 0.1 convert_element_type.25
  74.4 0.7 fusion
  (13 shorter events, 0.1 us)
Async XLA Ops:
  0.0 51.1 %copy-start = (f32[4]{0:T(128)S(1)}, f32[4]{0:T(128)}, u32[]{:S(2)}) copy-start(f32[4]{0:T(128)} %param.10) | copy-start | bytes 52
  0.0 51.1 %copy-start.1 = (s32[4]{0:T(128)S(1)}, s32[4]{0:T(128)}, u32[]{:S(2)}) copy-start(s32[4]{0:T(128)} %param.9) | copy-start | bytes 52
  0.0 54.4 %collective-permute-start.2 = (bf16[4,512,512]{2,1,0:T(8,128)(2,1)}, bf16[4,512,512]{2,1,0:T(8,128)(2,1)}, u32[]{:S(2)}, u32[]{:S(2)}) collective-permute-start(bf16[4,512,512]{2,1,0:T(8,128)(2,1)} %bitcast.22), channel_id=1, source_target_pairs={{0,1},{1,0},{2,3},{3,2},{4,5},{5,4},{6,7},{7,6},{8,9},{9,8},{10,11... | collective-permute-start | bytes 6291464 | tf_op jit(solution)/shard_map/ppermute | solution.py:186
  2.1 52.3 %collective-permute-start.1 = (bf16[4,512,512]{2,1,0:T(8,128)(2,1)}, bf16[4,512,512]{2,1,0:T(8,128)(2,1)}, u32[]{:S(2)}, u32[]{:S(2)}) collective-permute-start(bf16[4,512,512]{2,1,0:T(8,128)(2,1)} %bitcast.19), channel_id=1, source_target_pairs={{0,1},{1,0},{2,3},{3,2},{4,5},{5,4},{6,7},{7,6},{8,9},{9,8},{10,11... | collective-permute-start | bytes 6291464 | tf_op jit(solution)/shard_map/ppermute | solution.py:187
  6.2 26.9 %collective-permute-start.3 = (bf16[128,512]{1,0:T(8,128)(2,1)S(1)}, bf16[128,512]{1,0:T(8,128)(2,1)S(1)}, u32[]{:S(2)}, u32[]{:S(2)}) collective-permute-start(bf16[128,512]{1,0:T(8,128)(2,1)S(1)} %and_select_fusion.1), channel_id=1, source_target_pairs={{64,0},{66,2},{68,4},{70,6},{72,8},{74,10},{76,12},{78,14},{80,16}... | collective-permute-start | bytes 393224 | tf_op jit(solution)/shard_map/ppermute | solution.py:169
  21.3 11.8 %collective-permute-start.4 = (bf16[128,512]{1,0:T(8,128)(2,1)S(1)}, bf16[128,512]{1,0:T(8,128)(2,1)S(1)}, u32[]{:S(2)}, u32[]{:S(2)}) collective-permute-start(bf16[128,512]{1,0:T(8,128)(2,1)S(1)} %and_select_fusion.1), channel_id=1, source_target_pairs={{1,65},{3,67},{5,69},{7,71},{9,73},{11,75},{13,77},{15,79},{17,81}... | collective-permute-start | bytes 393224 | tf_op jit(solution)/shard_map/ppermute | solution.py:170
  23.2 15.5 %collective-permute-start.6 = (bf16[512,512]{1,0:T(8,128)(2,1)S(1)}, bf16[512,512]{1,0:T(8,128)(2,1)S(1)}, u32[]{:S(2)}, u32[]{:S(2)}) collective-permute-start(bf16[512,512]{1,0:T(8,128)(2,1)S(1)} %and_select_fusion.rest_4_), channel_id=1, source_target_pairs={{8,0},{10,2},{12,4},{14,6},{16,8},{1,9},{18,10},{3,11},{20,12},{5,... | collective-permute-start | bytes 1572872 | tf_op jit(solution)/shard_map/ppermute | solution.py:173
  33.9 15.2 %all-to-all-start = ((bf16[4,128,512]{2,1,0:T(8,128)(2,1)}), bf16[4,128,512]{2,1,0:T(8,128)(2,1)S(1)}, u32[]{:S(2)}, u32[]{:S(2)}) async-start(bf16[4,128,512]{2,1,0:T(8,128)(2,1)} %broadcast_in_dim.32), calls=%async_computation | async-start | bytes 1048576 | tf_op jit(solution)/shard_map/all_to_all | solution.py:196
  38.7 15.7 %collective-permute-start.7 = (bf16[512,512]{1,0:T(8,128)(2,1)S(1)}, bf16[512,512]{1,0:T(8,128)(2,1)S(1)}, u32[]{:S(2)}, u32[]{:S(2)}) collective-permute-start(bf16[512,512]{1,0:T(8,128)(2,1)S(1)} %collective-permute-done.6.rest_5_), channel_id=1, source_target_pairs={{0,1},{1,0},{2,3},{3,2},{4,5},{5,4},{6,7},{7,6},{8,9},{9,8},{10,11... | collective-permute-start | bytes 1572872 | tf_op jit(solution)/shard_map/ppermute | solution.py:189
  49.1 11.5 %collective-permute-start.5 = (bf16[512,512]{1,0:T(8,128)(2,1)S(1)}, bf16[512,512]{1,0:T(8,128)(2,1)S(1)}, u32[]{:S(2)}, u32[]{:S(2)}) collective-permute-start(bf16[512,512]{1,0:T(8,128)(2,1)S(1)} %bitcast.17), channel_id=1, source_target_pairs={{0,1},{1,0},{2,3},{3,2},{4,5},{5,4},{6,7},{7,6},{8,9},{9,8},{10,11... | collective-permute-start | bytes 1572872 | tf_op jit(solution)/shard_map/ppermute | solution.py:199
  51.2 3.2 %collective-permute-start = (f32[10]{0:T(128)S(1)}, f32[10]{0:T(128)S(1)}, u32[]{:S(2)}, u32[]{:S(2)}) collective-permute-start(f32[10]{0:T(128)S(1)} %compare_select_fusion.2.mine), channel_id=1, source_target_pairs={{0,1},{1,0},{2,3},{3,2},{4,5},{5,4},{6,7},{7,6},{8,9},{9,8},{10,11... | collective-permute-start | bytes 128 | tf_op jit(solution)/shard_map/ppermute | solution.py:188
